TPU v7x, 128 devices: a whole 4x4x4 slice. The times are simulated.
128 devices in a mesh: seq: 32 (over z, y_hi, x), grp: 4 (over y_lo, core).
Axes of the slice: x: 4, y: 4 (y_hi: 2, y_lo: 2; y = y_hi * 2 + y_lo), z: 4, core: 2. Of those that a mesh axis runs over, the one named last changes fastest.
Arguments:
- query_vecs: bfloat16 [65536, 1024], P(('seq', 'grp')), may hold values from -6 to 6
- key_vecs: bfloat16 [65536, 1024], P(('seq', 'grp')), may hold values from -6 to 6
- value_vecs: bfloat16 [65536, 1024], P(('seq', 'grp')), may hold values from -6 to 6
Outputs:
- attended: bfloat16 [65536, 1024], P(('seq', 'grp'))
All inputs are finite; a program needn't handle non-finite values.
Results may differ from a plain program's by a relative error of at most 0.0033.
Values may be sent and summed in bfloat16 or wider, within the bound.
A program may use at most 128 MiB of HBM per device.

v0:
```python
import math

import jax
import jax.numpy as jnp
from jax import lax
from jax.sharding import PartitionSpec as P

HEADS = 8
HEAD_DIM = 128
BLK = 256
LEV = 4


very_negative = -1e30


def from_behind(value, axis, steps):
    count = lax.axis_size(axis)
    initial, last = (max(0, -steps), min(count, count - steps))
    return lax.ppermute(value, axis, [(source, source + steps) for source in range(initial, last)])


def coarsen_heads(rows_in, factor):
    head_count, row_count, head_size = rows_in.shape
    paired = rows_in.reshape(head_count, row_count // 2, 2, head_size).astype(jnp.float32)
    return ((paired[:, :, 0] + paired[:, :, 1]) * factor).astype(jnp.bfloat16)


def block_terms(query_grp, key_grp, value_grp, height, own_first, block_total):
    group_size = query_grp.shape[1]
    block_rows = query_grp.shape[2]
    score_scale = 1.0 / math.sqrt(query_grp.shape[3])
    if height == 0:
        offsets = (0, 1, 2)
    else:
        offsets = (0, 2)
    place = jnp.arange(block_rows, dtype=jnp.int32)
    upper = place >= block_rows // 2
    lower = jnp.logical_not(upper)
    own_block = own_first + jnp.arange(group_size, dtype=jnp.int32)
    masks = []
    scored = []
    row_max = None
    for offset in offsets:
        scores = (
            jnp.einsum(
                "hgqd,hgkd->hgqk",
                query_grp,
                key_grp[:, offset : offset + group_size],
                preferred_element_type=jnp.float32,
            )
            * score_scale
        )
        other_block = own_block + (offset - 1)
        present = jnp.logical_and(other_block >= 0, other_block < block_total)
        allowed = jnp.broadcast_to(present[:, None, None], (group_size, block_rows, block_rows))
        if height > 0:
            if offset == 0:
                excluded = jnp.logical_and(lower[:, None], upper[None, :])
            else:
                excluded = jnp.logical_and(upper[:, None], lower[None, :])
            allowed = jnp.logical_and(allowed, jnp.logical_not(excluded)[None, :, :])
        allowed = allowed[None]
        masked = jnp.where(allowed, scores, very_negative)
        masks.append(allowed)
        scored.append(masked)
        part_max = jnp.max(masked, axis=-1)
        row_max = part_max if row_max is None else jnp.maximum(row_max, part_max)
    row_total = None
    weighted = None
    for allowed, masked, offset in zip(masks, scored, offsets):
        weights = jnp.where(allowed, jnp.exp(masked - row_max[..., None]), 0.0)
        part_total = jnp.sum(weights, axis=-1)
        part_sum = jnp.einsum(
            "hgqk,hgkd->hgqd",
            weights.astype(jnp.bfloat16),
            value_grp[:, offset : offset + group_size],
            preferred_element_type=jnp.float32,
        )
        row_total = part_total if row_total is None else row_total + part_total
        weighted = part_sum if weighted is None else weighted + part_sum
    return (row_max, weighted, row_total * 2.0**height)


def level_stats(query_rows, key_rows, value_rows, height, grouped):
    head_count, row_count, head_size = query_rows.shape
    block_count = row_count // BLK
    head_part = jnp.stack([key_rows[:, :BLK], value_rows[:, :BLK]])
    tail_part = jnp.stack([key_rows[:, row_count - BLK :], value_rows[:, row_count - BLK :]])
    if grouped:
        from_left = from_behind(tail_part, "seq", 1)
        from_right = from_behind(head_part, "seq", -1)
        first_block = lax.axis_index("seq") * block_count
        block_total = lax.axis_size("seq") * block_count
    else:
        from_left = from_behind(tail_part, ("seq", "grp"), 1)
        from_right = from_behind(head_part, ("seq", "grp"), -1)
        first_block = lax.axis_index(("seq", "grp")) * block_count
        block_total = lax.axis_size(("seq", "grp")) * block_count
    key_pad = jnp.concatenate([from_left[0], key_rows, from_right[0]], axis=1).reshape(
        head_count, block_count + 2, BLK, head_size
    )
    value_pad = jnp.concatenate([from_left[1], value_rows, from_right[1]], axis=1).reshape(
        head_count, block_count + 2, BLK, head_size
    )
    query_blocks = query_rows.reshape(head_count, block_count, BLK, head_size)
    row_max, weighted, row_total = block_terms(
        query_blocks, key_pad, value_pad, height, first_block, block_total
    )
    return (
        row_max.reshape(head_count, row_count),
        weighted.reshape(head_count, row_count, head_size),
        row_total.reshape(head_count, row_count),
    )


def merge_stats(finer, coarser):
    fine_max, fine_sum, fine_total = finer
    coarse_max, coarse_sum, coarse_total = coarser
    both_max = jnp.maximum(fine_max, coarse_max)
    fine_factor = jnp.exp(fine_max - both_max)
    coarse_factor = jnp.exp(coarse_max - both_max)
    merged = fine_sum * fine_factor[..., None] + coarse_sum * coarse_factor[..., None]
    return (both_max, merged, fine_total * fine_factor + coarse_total * coarse_factor)


def widen_stats(stats):
    return tuple((jnp.repeat(member, 2, axis=1) for member in stats))


def merge_down(stats_list):
    running = stats_list[-1]
    running = merge_stats(stats_list[0], widen_stats(running))
    return running


def to_heads(rows_in):
    row_count = rows_in.shape[0]
    return jnp.transpose(rows_in.reshape(row_count, HEADS, HEAD_DIM), (1, 0, 2))


def finish_output(stats):
    row_max, weighted, row_total = stats
    head_count, row_count, head_size = weighted.shape
    result = weighted / row_total[..., None]
    return (
        jnp.transpose(result, (1, 0, 2))
        .reshape(row_count, head_count * head_size)
        .astype(jnp.bfloat16)
    )


def local(query_vecs, key_vecs, value_vecs):
    row_count = query_vecs.shape[0]
    fine_count = 0
    while (
        fine_count < LEV
        and row_count >> fine_count >= BLK
        and ((row_count >> fine_count) % BLK == 0)
    ):
        fine_count = fine_count + 1
    query_rows = to_heads(query_vecs)
    key_rows = to_heads(key_vecs)
    value_rows = to_heads(value_vecs)
    fine_stats = []
    for height in range(fine_count):
        if height > 0:
            query_rows = coarsen_heads(query_rows, 0.5)
            key_rows = coarsen_heads(key_rows, 0.5)
            value_rows = coarsen_heads(value_rows, 1.0)
        fine_stats.append(level_stats(query_rows, key_rows, value_rows, height, False))
    coarse_stats = []
    for height in range(fine_count, LEV):
        query_rows = coarsen_heads(query_rows, 0.5)
        key_rows = coarsen_heads(key_rows, 0.5)
        value_rows = coarsen_heads(value_rows, 1.0)
        group_query, group_key, group_value = (
            lax.all_to_all(query_rows, "grp", split_axis=0, concat_axis=1, tiled=True),
            lax.all_to_all(key_rows, "grp", split_axis=0, concat_axis=1, tiled=True),
            lax.all_to_all(value_rows, "grp", split_axis=0, concat_axis=1, tiled=True),
        )
        local_max, local_sum, local_total = level_stats(
            group_query, group_key, group_value, height, True
        )
        coarse_stats.append(
            (
                lax.all_to_all(local_max, "grp", split_axis=1, concat_axis=0, tiled=True),
                lax.all_to_all(local_sum, "grp", split_axis=1, concat_axis=0, tiled=True),
                lax.all_to_all(local_total, "grp", split_axis=1, concat_axis=0, tiled=True),
            )
        )
    running = merge_down(coarse_stats)
    for height in range(fine_count - 1, -1, -1):
        running = merge_stats(fine_stats[height], widen_stats(running))
    return finish_output(running)


def solution(mesh):
    return jax.shard_map(
        local,
        mesh=mesh,
        in_specs=(P(("seq", "grp"), None), P(("seq", "grp"), None), P(("seq", "grp"), None)),
        out_specs=P(("seq", "grp"), None),
        check_vma=False,
    )
```

profile of v0, /device:TPU:97, one launch (start us, length us, event | category | flops | bytes accessed | tf_op | source)
XLA Modules:
  0.0 229.6 jit_solution(1742466582472509571)
XLA Ops:
  0.0 1.6 copy.605
  4.2 2.6 %collective-permute-start.3 = (bf16[2,8,256,128]{3,1,2,0:T(8,128)(2,1)}, bf16[2,8,256,128]{3,1,2,0:T(8,128)(2,1)}, u32[]{:S(2)}, u32[]{:S(2)}) collective-permute-start(bf16[2,8,256,128]{3,1,2,0:T(8,128)(2,1)} %pad_maximum_fusion.6), channel_id=1, source_target_pairs={{1,0},{2,1},{3,2},{4,3},{5,4},{6,5},{7,6},{8,7},{9,8},{10,9},{11,1... | collective-permute-start | bytes 3145736 | tf_op jit(solution)/shard_map/ppermute | solution.py:20
  6.8 3.1 %collective-permute-start.2 = (bf16[2,8,256,128]{3,1,2,0:T(8,128)(2,1)}, bf16[2,8,256,128]{3,1,2,0:T(8,128)(2,1)}, u32[]{:S(2)}, u32[]{:S(2)}) collective-permute-start(bf16[2,8,256,128]{3,1,2,0:T(8,128)(2,1)} %pad_maximum_fusion.6), channel_id=1, source_target_pairs={{0,1},{1,2},{2,3},{3,4},{4,5},{5,6},{6,7},{7,8},{8,9},{9,10},{10,1... | collective-permute-start | bytes 3145736 | tf_op jit(solution)/shard_map/ppermute | solution.py:20
  13.2 6.6 %all-to-all-start.6 = ((bf16[8,64,128]{2,1,0:T(8,128)(2,1)}), bf16[8,64,128]{2,1,0:T(8,128)(2,1)S(1)}, u32[]{:S(2)}, u32[]{:S(2)}) async-start(bf16[8,64,128]{2,1,0:T(8,128)(2,1)} %fusion.111), calls=%async_computation.6 | async-start | bytes 262144 | tf_op jit(solution)/shard_map/all_to_all | solution.py:180
  19.8 2.3 %slice_bitcast_fusion.12 = (bf16[1,8,256,128]{3,1,2,0:T(8,128)(2,1)}, bf16[1,8,256,128]{3,1,2,0:T(8,128)(2,1)S(1)}, bf16[1,8,256,128]{3,1,2,0:T(8,128)(2,1)S(1)}, bf16[1,8,256,128]{3,1,2,0:T(8,128)(2,1)}) fusion(bf16[8,512,128]{2,0,1:T(8,128)(2,1)} %bitcast.304, bf16[8,512,128]{2,0,1:T(8,128)(2,1)S(1)} %bitcast.301), kind=kLoop, calls=%fused_computation.111 | loop fusion | bytes 4194304 | tf_op jit(solution)/shard_map/stack | solution.py:89
  23.2 1.9 collective-permute-start.1
  25.2 2.4 %fusion.154 = bf16[8,256,128]{2,0,1:T(8,128)(2,1)} fusion(f32[8,256,2,128]{3,0,2,1:T(8,128)} %copy-done.2), kind=kLoop, calls=%fused_computation.249 | loop fusion | flops 524288 | bytes 2621440 | tf_op jit(solution)/shard_map/convert_element_type | solution.py:26
  38.1 6.6 %all-to-all-done.6 = bf16[8,64,128]{2,1,0:T(8,128)(2,1)S(1)} async-done(((bf16[8,64,128]{2,1,0:T(8,128)(2,1)}), bf16[8,64,128]{2,1,0:T(8,128)(2,1)S(1)}, u32[]{:S(2)}, u32[]{:S(2)}) %all-to-all-start.6) | async-done | bytes 131104 | tf_op jit(solution)/shard_map/all_to_all | solution.py:180
  44.8 3.7 %all-to-all-start.5 = ((bf16[8,64,128]{2,1,0:T(8,128)(2,1)}), bf16[8,64,128]{2,1,0:T(8,128)(2,1)S(1)}, u32[]{:S(2)}, u32[]{:S(2)}) async-start(bf16[8,64,128]{2,1,0:T(8,128)(2,1)} %fusion.110), calls=%async_computation.5 | async-start | bytes 262144 | tf_op jit(solution)/shard_map/all_to_all | solution.py:179
  48.5 3.6 %all-to-all-done.5 = bf16[8,64,128]{2,1,0:T(8,128)(2,1)S(1)} async-done(((bf16[8,64,128]{2,1,0:T(8,128)(2,1)}), bf16[8,64,128]{2,1,0:T(8,128)(2,1)S(1)}, u32[]{:S(2)}, u32[]{:S(2)}) %all-to-all-start.5) | async-done | bytes 131104 | tf_op jit(solution)/shard_map/all_to_all | solution.py:179
  52.1 4.3 %all-to-all-start.4 = ((bf16[8,64,128]{2,1,0:T(8,128)(2,1)}), bf16[8,64,128]{2,1,0:T(8,128)(2,1)S(1)}, u32[]{:S(2)}, u32[]{:S(2)}) async-start(bf16[8,64,128]{2,1,0:T(8,128)(2,1)} %fusion.109), calls=%async_computation.4 | async-start | bytes 262144 | tf_op jit(solution)/shard_map/all_to_all | solution.py:178
  56.4 3.6 %all-to-all-done.4 = bf16[8,64,128]{2,1,0:T(8,128)(2,1)S(1)} async-done(((bf16[8,64,128]{2,1,0:T(8,128)(2,1)}), bf16[8,64,128]{2,1,0:T(8,128)(2,1)S(1)}, u32[]{:S(2)}, u32[]{:S(2)}) %all-to-all-start.4) | async-done | bytes 131104 | tf_op jit(solution)/shard_map/all_to_all | solution.py:178
  60.0 4.4 %all-to-all-start.2 = ((bf16[8,128,128]{2,1,0:T(8,128)(2,1)}), bf16[8,128,128]{2,1,0:T(8,128)(2,1)S(1)}, u32[]{:S(2)}, u32[]{:S(2)}) async-start(bf16[8,128,128]{2,1,0:T(8,128)(2,1)} %bitcast.51), calls=%async_computation.2 | async-start | bytes 524288 | tf_op jit(solution)/shard_map/all_to_all | solution.py:180
  65.3 4.2 %all-to-all-done.2 = bf16[8,128,128]{2,1,0:T(8,128)(2,1)S(1)} async-done(((bf16[8,128,128]{2,1,0:T(8,128)(2,1)}), bf16[8,128,128]{2,1,0:T(8,128)(2,1)S(1)}, u32[]{:S(2)}, u32[]{:S(2)}) %all-to-all-start.2) | async-done | bytes 262176 | tf_op jit(solution)/shard_map/all_to_all | solution.py:180
  69.5 4.3 %all-to-all-start.1 = ((bf16[8,128,128]{2,1,0:T(8,128)(2,1)}), bf16[8,128,128]{2,1,0:T(8,128)(2,1)S(1)}, u32[]{:S(2)}, u32[]{:S(2)}) async-start(bf16[8,128,128]{2,1,0:T(8,128)(2,1)} %bitcast.44), calls=%async_computation.1 | async-start | bytes 524288 | tf_op jit(solution)/shard_map/all_to_all | solution.py:179
  75.6 1.9 collective-permute-start.7
  77.6 3.4 %collective-permute-start.6 = (bf16[2,2,256,128]{3,2,1,0:T(8,128)(2,1)}, bf16[2,2,256,128]{3,2,1,0:T(8,128)(2,1)S(1)}, u32[]{:S(2)}, u32[]{:S(2)}) collective-permute-start(bf16[2,2,256,128]{3,2,1,0:T(8,128)(2,1)} %pad_maximum_fusion.13), channel_id=1, source_target_pairs={{0,4},{4,8},{8,12},{12,16},{16,20},{20,24},{24,28},{28,32},{32,36}... | collective-permute-start | bytes 786440 | tf_op jit(solution)/shard_map/ppermute | solution.py:20
  81.0 4.0 %all-to-all-start = ((bf16[8,128,128]{2,1,0:T(8,128)(2,1)}), bf16[8,128,128]{2,1,0:T(8,128)(2,1)S(1)}, u32[]{:S(2)}, u32[]{:S(2)}) async-start(bf16[8,128,128]{2,1,0:T(8,128)(2,1)} %bitcast.38), calls=%async_computation | async-start | bytes 524288 | tf_op jit(solution)/shard_map/all_to_all | solution.py:178
  86.5 8.2 %all-to-all-done = bf16[8,128,128]{2,1,0:T(8,128)(2,1)S(1)} async-done(((bf16[8,128,128]{2,1,0:T(8,128)(2,1)}), bf16[8,128,128]{2,1,0:T(8,128)(2,1)S(1)}, u32[]{:S(2)}, u32[]{:S(2)}) %all-to-all-start) | async-done | bytes 262176 | tf_op jit(solution)/shard_map/all_to_all | solution.py:178
  95.5 2.0 collective-permute-start.5
  98.5 3.4 %collective-permute-start.4 = (bf16[2,2,256,128]{3,2,1,0:T(8,128)(2,1)}, bf16[2,2,256,128]{3,2,1,0:T(8,128)(2,1)}, u32[]{:S(2)}, u32[]{:S(2)}) collective-permute-start(bf16[2,2,256,128]{3,2,1,0:T(8,128)(2,1)} %pad_maximum_fusion.11), channel_id=1, source_target_pairs={{0,4},{4,8},{8,12},{12,16},{16,20},{20,24},{24,28},{28,32},{32,36}... | collective-permute-start | bytes 786440 | tf_op jit(solution)/shard_map/ppermute | solution.py:20
  106.7 4.2 %all-to-all-start.11 = ((f32[4,1,128]{2,1,0:T(1,128)}), f32[4,1,128]{2,1,0:T(1,128)S(1)}, u32[]{:S(2)}, u32[]{:S(2)}) async-start(f32[4,1,128]{2,1,0:T(1,128)} %reshape.884), calls=%async_computation.11 | async-start | bytes 4096 | tf_op jit(solution)/shard_map/all_to_all | solution.py:189
  110.9 3.5 %collective-permute-start = (bf16[2,8,256,128]{3,1,2,0:T(8,128)(2,1)}, bf16[2,8,256,128]{3,1,2,0:T(8,128)(2,1)}, u32[]{:S(2)}, u32[]{:S(2)}) collective-permute-start(bf16[2,8,256,128]{3,1,2,0:T(8,128)(2,1)} %pad_maximum_fusion.4), channel_id=1, source_target_pairs={{0,1},{1,2},{2,3},{3,4},{4,5},{5,6},{6,7},{7,8},{8,9},{9,10},{10,1... | collective-permute-start | bytes 3145736 | tf_op jit(solution)/shard_map/ppermute | solution.py:20
  114.5 1.6 slice_bitcast_fusion.20
  116.1 1.6 slice_bitcast_fusion.21
  120.0 3.8 %all-to-all-start.7 = ((f32[4,1,128]{2,1,0:T(1,128)}), f32[4,1,128]{2,1,0:T(1,128)}, u32[]{:S(2)}, u32[]{:S(2)}) async-start(f32[4,1,128]{2,1,0:T(1,128)} %reshape.882), calls=%async_computation.7 | async-start | bytes 4096 | tf_op jit(solution)/shard_map/all_to_all | solution.py:187
  124.5 2.0 all-to-all-done.7
  126.5 4.1 %all-to-all-start.10 = ((f32[2,4,128]{2,0,1:T(2,128)}), f32[2,4,128]{2,0,1:T(2,128)S(1)}, u32[]{:S(2)}, u32[]{:S(2)}) async-start(f32[2,4,128]{2,0,1:T(2,128)} %copy.558), calls=%async_computation.10 | async-start | bytes 8192 | tf_op jit(solution)/shard_map/all_to_all | solution.py:189
  130.7 1.8 pad_maximum_fusion.8
  133.8 3.9 %all-to-all-start.3 = ((f32[2,4,128]{2,0,1:T(2,128)}), f32[2,4,128]{2,0,1:T(2,128)S(1)}, u32[]{:S(2)}, u32[]{:S(2)}) async-start(f32[2,4,128]{2,0,1:T(2,128)} %copy.519), calls=%async_computation.3 | async-start | bytes 8192 | tf_op jit(solution)/shard_map/all_to_all | solution.py:187
  137.7 2.3 fusion.74
  140.6 4.1 %all-to-all-start.9 = ((f32[2,256,128]{2,0,1:T(2,128)}), f32[2,256,128]{2,0,1:T(2,128)S(1)}, u32[]{:S(2)}, u32[]{:S(2)}) async-start(f32[2,256,128]{2,0,1:T(2,128)} %copy.552), calls=%async_computation.9 | async-start | bytes 524288 | tf_op jit(solution)/shard_map/all_to_all | solution.py:188
  144.7 1.6 convolution_add_fusion.1
  147.5 2.2 all-to-all-done.9
  149.7 4.4 %all-to-all-start.8 = ((f32[2,512,128]{2,0,1:T(2,128)}), f32[2,512,128]{2,0,1:T(2,128)S(1)}, u32[]{:S(2)}, u32[]{:S(2)}) async-start(f32[2,512,128]{2,0,1:T(2,128)} %copy.545), calls=%async_computation.8 | async-start | bytes 1048576 | tf_op jit(solution)/shard_map/all_to_all | solution.py:188
  158.8 3.2 %all-to-all-done.8 = f32[2,512,128]{2,0,1:T(2,128)S(1)} async-done(((f32[2,512,128]{2,0,1:T(2,128)}), f32[2,512,128]{2,0,1:T(2,128)S(1)}, u32[]{:S(2)}, u32[]{:S(2)}) %all-to-all-start.8) | async-done | bytes 524320 | tf_op jit(solution)/shard_map/all_to_all | solution.py:188
  177.3 2.3 fusion.132
  180.8 1.8 fusion.44
  184.4 1.7 copy.497
  187.6 2.9 %fusion.140 = (f32[8,2,256]{2,1,0:T(2,128)S(1)}, f32[8,2,256,256]{3,2,1,0:T(8,128)}) fusion(bf16[8,4,256,128]{3,2,1,0:T(8,128)(2,1)S(1)} %bitcast.328, bf16[8,2,256,128]{3,0,2,1:T(8,128)(2,1)S(1)} %bitcast.314, pred[2]{0:T(512)(128)(4,1)S(1)} %copy-done.42), kind=kOutput, calls=%fused_computation.240 | convolution fusion | flops 271577088 | bytes 7356418 | tf_op jit(solution)/shard_map/hgqd,hgkd->hgqk/dot_general | solution.py:46
  190.5 5.4 %copy.501 = f32[8,2,256,256]{2,3,1,0:T(8,128)} copy(f32[8,2,256,256]{3,2,1,0:T(8,128)} %get-tuple-element.72) | data formatting | bytes 8388608 | tf_op jit(solution)/shard_map/jit(_where)/select_n | solution.py:64
  195.8 4.3 %fusion.141 = (f32[8,2,256]{2,1,0:T(2,128)S(1)}, f32[8,2,256,256]{3,2,1,0:T(8,128)}) fusion(bf16[8,4,256,128]{3,2,1,0:T(8,128)(2,1)} %bitcast.329, bf16[8,2,256,128]{3,0,2,1:T(8,128)(2,1)S(1)} %bitcast.315, pred[2]{0:T(512)(128)(4,1)S(1)} %copy-done.40), kind=kOutput, calls=%fused_computation.241 | convolution fusion | flops 271577088 | bytes 7356418 | tf_op jit(solution)/shard_map/hgqd,hgkd->hgqk/dot_general | solution.py:46
  201.0 2.3 %copy-done.1 = f32[8,2,256,256]{2,3,1,0:T(8,128)S(1)} copy-done((f32[8,2,256,256]{2,3,1,0:T(8,128)S(1)}, f32[8,2,256,256]{2,3,1,0:T(8,128)}, u32[]{:S(2)}) %copy-start.1) | copy-done | bytes 4194328
  204.5 2.4 %fusion.10 = f32[8,2,256,128]{3,2,1,0:T(8,128)} fusion(f32[8,2,256,256]{2,3,1,0:T(8,128)S(1)} %copy-done.1, f32[8,2,256]{2,1,0:T(2,128)S(1)} %bitcast.362, pred[2]{0:T(512)(128)(4,1)S(1)} %copy-done.42, bf16[8,4,256,128]{3,2,1,0:T(8,128)(2,1)S(1)} %bitcast.307), kind=kOutput, calls=%fused_computation.16 | convolution fusion | flops 271581184 | bytes 7356928 | tf_op jit(solution)/shard_map/hgqk,hgkd->hgqd/dot_general | solution.py:74
  206.9 2.7 %fusion.8 = f32[8,2,256,128]{3,2,1,0:T(8,128)} fusion(f32[8,2,256,256]{3,2,1,0:T(8,128)S(1)} %get-tuple-element.74, f32[8,2,256]{2,1,0:T(2,128)S(1)} %bitcast.363, pred[2]{0:T(512)(128)(4,1)S(1)} %copy-done.41, bf16[8,4,256,128]{3,2,1,0:T(8,128)(2,1)S(1)} %bitcast.308), kind=kOutput, calls=%fused_computation.15 | convolution fusion | flops 273678336 | bytes 7357440 | tf_op jit(solution)/shard_map/hgqk,hgkd->hgqd/dot_general | solution.py:74
  209.6 5.4 %copy.499 = f32[8,2,256,256]{2,3,1,0:T(8,128)} copy(f32[8,2,256,256]{3,2,1,0:T(8,128)} %get-tuple-element.76) | data formatting | bytes 8388608 | tf_op jit(solution)/shard_map/jit(_where)/select_n | solution.py:64
  214.9 6.1 %fusion.2 = (f32[8,2,256]{2,1,0:T(2,128)S(1)}, f32[8,2,256]{2,1,0:T(2,128)S(1)}, f32[8,2,256]{2,1,0:T(2,128)S(1)}) fusion(f32[8,2,256,256]{2,3,1,0:T(8,128)} %copy.499, f32[8,2,256]{2,1,0:T(2,128)S(1)} %bitcast.364, pred[2]{0:T(512)(128)(4,1)S(1)} %copy-done.40, f32[8,2,256,256]{2,3,1,0:T(8,128)} %copy.501, pred[2]{0:T(512)(128)(4,1)S(1)} %copy-done.42, ...), kind=kLoop, calls=%fused_computation.9 | loop fusion | flops 11522048 | bytes 12648454 | tf_op jit(solution)/shard_map/reduce_sum | solution.py:73
  226.4 2.1 fusion.18
  (228 shorter events, 66.6 us)
Async XLA Ops:
  2.1 7.8 %copy-start.2 = (f32[8,256,2,128]{3,0,2,1:T(8,128)}, f32[8,256,2,128]{3,0,2,1:T(8,128)S(1)}, u32[]{:S(2)}) copy-start(f32[8,256,2,128]{3,0,2,1:T(8,128)S(1)} %convert.11) | copy-start | bytes 6291460
  4.2 159.3 %collective-permute-start.3 = (bf16[2,8,256,128]{3,1,2,0:T(8,128)(2,1)}, bf16[2,8,256,128]{3,1,2,0:T(8,128)(2,1)}, u32[]{:S(2)}, u32[]{:S(2)}) collective-permute-start(bf16[2,8,256,128]{3,1,2,0:T(8,128)(2,1)} %pad_maximum_fusion.6), channel_id=1, source_target_pairs={{1,0},{2,1},{3,2},{4,3},{5,4},{6,5},{7,6},{8,7},{9,8},{10,9},{11,1... | collective-permute-start | bytes 3145736 | tf_op jit(solution)/shard_map/ppermute | solution.py:20
  6.8 158.0 %collective-permute-start.2 = (bf16[2,8,256,128]{3,1,2,0:T(8,128)(2,1)}, bf16[2,8,256,128]{3,1,2,0:T(8,128)(2,1)}, u32[]{:S(2)}, u32[]{:S(2)}) collective-permute-start(bf16[2,8,256,128]{3,1,2,0:T(8,128)(2,1)} %pad_maximum_fusion.6), channel_id=1, source_target_pairs={{0,1},{1,2},{2,3},{3,4},{4,5},{5,6},{6,7},{7,8},{8,9},{9,10},{10,1... | collective-permute-start | bytes 3145736 | tf_op jit(solution)/shard_map/ppermute | solution.py:20
  13.2 31.6 %all-to-all-start.6 = ((bf16[8,64,128]{2,1,0:T(8,128)(2,1)}), bf16[8,64,128]{2,1,0:T(8,128)(2,1)S(1)}, u32[]{:S(2)}, u32[]{:S(2)}) async-start(bf16[8,64,128]{2,1,0:T(8,128)(2,1)} %fusion.111), calls=%async_computation.6 | async-start | bytes 262144 | tf_op jit(solution)/shard_map/all_to_all | solution.py:180
  23.2 156.3 %collective-permute-start.1 = (bf16[2,8,256,128]{3,1,2,0:T(8,128)(2,1)}, bf16[2,8,256,128]{3,1,2,0:T(8,128)(2,1)}, u32[]{:S(2)}, u32[]{:S(2)}) collective-permute-start(bf16[2,8,256,128]{3,1,2,0:T(8,128)(2,1)} %pad_maximum_fusion.5), channel_id=1, source_target_pairs={{1,0},{2,1},{3,2},{4,3},{5,4},{6,5},{7,6},{8,7},{9,8},{10,9},{11,1... | collective-permute-start | bytes 3145736 | tf_op jit(solution)/shard_map/ppermute | solution.py:20
  35.8 38.0 %copy-start.20 = (bf16[1,8,256,128]{3,1,2,0:T(8,128)(2,1)S(1)}, bf16[1,8,256,128]{3,1,2,0:T(8,128)(2,1)}, u32[]{:S(2)}) copy-start(bf16[1,8,256,128]{3,1,2,0:T(8,128)(2,1)} %get-tuple-element.43) | copy-start | bytes 1572868
  35.8 37.9 %copy-start.21 = (bf16[1,8,256,128]{3,1,2,0:T(8,128)(2,1)S(1)}, bf16[1,8,256,128]{3,1,2,0:T(8,128)(2,1)}, u32[]{:S(2)}) copy-start(bf16[1,8,256,128]{3,1,2,0:T(8,128)(2,1)} %get-tuple-element.92) | copy-start | bytes 1572868
  44.8 7.3 %all-to-all-start.5 = ((bf16[8,64,128]{2,1,0:T(8,128)(2,1)}), bf16[8,64,128]{2,1,0:T(8,128)(2,1)S(1)}, u32[]{:S(2)}, u32[]{:S(2)}) async-start(bf16[8,64,128]{2,1,0:T(8,128)(2,1)} %fusion.110), calls=%async_computation.5 | async-start | bytes 262144 | tf_op jit(solution)/shard_map/all_to_all | solution.py:179
  52.1 7.9 %all-to-all-start.4 = ((bf16[8,64,128]{2,1,0:T(8,128)(2,1)}), bf16[8,64,128]{2,1,0:T(8,128)(2,1)S(1)}, u32[]{:S(2)}, u32[]{:S(2)}) async-start(bf16[8,64,128]{2,1,0:T(8,128)(2,1)} %fusion.109), calls=%async_computation.4 | async-start | bytes 262144 | tf_op jit(solution)/shard_map/all_to_all | solution.py:178
  60.0 9.5 %all-to-all-start.2 = ((bf16[8,128,128]{2,1,0:T(8,128)(2,1)}), bf16[8,128,128]{2,1,0:T(8,128)(2,1)S(1)}, u32[]{:S(2)}, u32[]{:S(2)}) async-start(bf16[8,128,128]{2,1,0:T(8,128)(2,1)} %bitcast.51), calls=%async_computation.2 | async-start | bytes 524288 | tf_op jit(solution)/shard_map/all_to_all | solution.py:180
  69.5 11.5 %all-to-all-start.1 = ((bf16[8,128,128]{2,1,0:T(8,128)(2,1)}), bf16[8,128,128]{2,1,0:T(8,128)(2,1)S(1)}, u32[]{:S(2)}, u32[]{:S(2)}) async-start(bf16[8,128,128]{2,1,0:T(8,128)(2,1)} %bitcast.44), calls=%async_computation.1 | async-start | bytes 524288 | tf_op jit(solution)/shard_map/all_to_all | solution.py:179
  75.6 19.8 %collective-permute-start.7 = (bf16[2,2,256,128]{3,2,1,0:T(8,128)(2,1)}, bf16[2,2,256,128]{3,2,1,0:T(8,128)(2,1)}, u32[]{:S(2)}, u32[]{:S(2)}) collective-permute-start(bf16[2,2,256,128]{3,2,1,0:T(8,128)(2,1)} %pad_maximum_fusion.13), channel_id=1, source_target_pairs={{4,0},{8,4},{12,8},{16,12},{20,16},{24,20},{28,24},{32,28},{36,32}... | collective-permute-start | bytes 786440 | tf_op jit(solution)/shard_map/ppermute | solution.py:20
  77.6 21.0 %collective-permute-start.6 = (bf16[2,2,256,128]{3,2,1,0:T(8,128)(2,1)}, bf16[2,2,256,128]{3,2,1,0:T(8,128)(2,1)S(1)}, u32[]{:S(2)}, u32[]{:S(2)}) collective-permute-start(bf16[2,2,256,128]{3,2,1,0:T(8,128)(2,1)} %pad_maximum_fusion.13), channel_id=1, source_target_pairs={{0,4},{4,8},{8,12},{12,16},{16,20},{20,24},{24,28},{28,32},{32,36}... | collective-permute-start | bytes 786440 | tf_op jit(solution)/shard_map/ppermute | solution.py:20
  80.9 21.0 %copy-start.34 = (bf16[2,4,64,128]{3,2,1,0:T(8,128)(2,1)}, bf16[2,4,64,128]{3,2,1,0:T(8,128)(2,1)S(1)}, u32[]{:S(2)}) copy-start(bf16[2,4,64,128]{3,2,1,0:T(8,128)(2,1)S(1)} %copy.522) | copy-start | bytes 393220
  81.0 13.8 %all-to-all-start = ((bf16[8,128,128]{2,1,0:T(8,128)(2,1)}), bf16[8,128,128]{2,1,0:T(8,128)(2,1)S(1)}, u32[]{:S(2)}, u32[]{:S(2)}) async-start(bf16[8,128,128]{2,1,0:T(8,128)(2,1)} %bitcast.38), calls=%async_computation | async-start | bytes 524288 | tf_op jit(solution)/shard_map/all_to_all | solution.py:178
  85.0 17.0 %copy-start.27 = (pred[256,256]{0,1:T(8,128)(4,1)S(1)}, pred[256,256]{0,1:T(8,128)(4,1)}, u32[]{:S(2)}) copy-start(pred[256,256]{0,1:T(8,128)(4,1)} %get-tuple-element.65) | copy-start | bytes 196612
  85.1 17.2 %copy-start.29 = (pred[256,256]{0,1:T(8,128)(4,1)S(1)}, pred[256,256]{0,1:T(8,128)(4,1)}, u32[]{:S(2)}) copy-start(pred[256,256]{0,1:T(8,128)(4,1)} %get-tuple-element.68) | copy-start | bytes 196612
  95.5 8.0 %copy-start.30 = (pred[256,256]{0,1:T(8,128)(4,1)S(1)}, pred[256,256]{0,1:T(8,128)(4,1)}, u32[]{:S(2)}) copy-start(pred[256,256]{0,1:T(8,128)(4,1)} %get-tuple-element.68) | copy-start | bytes 196612
  95.5 15.5 %collective-permute-start.5 = (bf16[2,2,256,128]{3,2,1,0:T(8,128)(2,1)}, bf16[2,2,256,128]{3,2,1,0:T(8,128)(2,1)}, u32[]{:S(2)}, u32[]{:S(2)}) collective-permute-start(bf16[2,2,256,128]{3,2,1,0:T(8,128)(2,1)} %pad_maximum_fusion.12), channel_id=1, source_target_pairs={{4,0},{8,4},{12,8},{16,12},{20,16},{24,20},{28,24},{32,28},{36,32}... | collective-permute-start | bytes 786440 | tf_op jit(solution)/shard_map/ppermute | solution.py:20
  98.5 17.6 %collective-permute-start.4 = (bf16[2,2,256,128]{3,2,1,0:T(8,128)(2,1)}, bf16[2,2,256,128]{3,2,1,0:T(8,128)(2,1)}, u32[]{:S(2)}, u32[]{:S(2)}) collective-permute-start(bf16[2,2,256,128]{3,2,1,0:T(8,128)(2,1)} %pad_maximum_fusion.11), channel_id=1, source_target_pairs={{0,4},{4,8},{8,12},{12,16},{16,20},{20,24},{24,28},{28,32},{32,36}... | collective-permute-start | bytes 786440 | tf_op jit(solution)/shard_map/ppermute | solution.py:20
  101.9 1.8 copy-start.28
  104.1 13.7 %copy-start.33 = (bf16[2,4,128,128]{3,2,1,0:T(8,128)(2,1)S(1)}, bf16[2,4,128,128]{3,2,1,0:T(8,128)(2,1)}, u32[]{:S(2)}) copy-start(bf16[2,4,128,128]{3,2,1,0:T(8,128)(2,1)} %copy.512) | copy-start | bytes 786436
  106.7 13.2 %all-to-all-start.11 = ((f32[4,1,128]{2,1,0:T(1,128)}), f32[4,1,128]{2,1,0:T(1,128)S(1)}, u32[]{:S(2)}, u32[]{:S(2)}) async-start(f32[4,1,128]{2,1,0:T(1,128)} %reshape.884), calls=%async_computation.11 | async-start | bytes 4096 | tf_op jit(solution)/shard_map/all_to_all | solution.py:189
  110.9 71.7 %collective-permute-start = (bf16[2,8,256,128]{3,1,2,0:T(8,128)(2,1)}, bf16[2,8,256,128]{3,1,2,0:T(8,128)(2,1)}, u32[]{:S(2)}, u32[]{:S(2)}) collective-permute-start(bf16[2,8,256,128]{3,1,2,0:T(8,128)(2,1)} %pad_maximum_fusion.4), channel_id=1, source_target_pairs={{0,1},{1,2},{2,3},{3,4},{4,5},{5,6},{6,7},{7,8},{8,9},{9,10},{10,1... | collective-permute-start | bytes 3145736 | tf_op jit(solution)/shard_map/ppermute | solution.py:20
  117.7 1.8 copy-start.22
  120.0 3.9 %copy-start.38 = (f32[4,1,128]{2,1,0:T(1,128)}, f32[4,1,128]{2,1,0:T(1,128)S(1)}, u32[]{:S(2)}) copy-start(f32[4,1,128]{2,1,0:T(1,128)S(1)} %all-to-all-done.11) | copy-start | bytes 6148
  120.0 6.5 %all-to-all-start.7 = ((f32[4,1,128]{2,1,0:T(1,128)}), f32[4,1,128]{2,1,0:T(1,128)}, u32[]{:S(2)}, u32[]{:S(2)}) async-start(f32[4,1,128]{2,1,0:T(1,128)} %reshape.882), calls=%async_computation.7 | async-start | bytes 4096 | tf_op jit(solution)/shard_map/all_to_all | solution.py:187
  126.5 7.2 %all-to-all-start.10 = ((f32[2,4,128]{2,0,1:T(2,128)}), f32[2,4,128]{2,0,1:T(2,128)S(1)}, u32[]{:S(2)}, u32[]{:S(2)}) async-start(f32[2,4,128]{2,0,1:T(2,128)} %copy.558), calls=%async_computation.10 | async-start | bytes 8192 | tf_op jit(solution)/shard_map/all_to_all | solution.py:189
  133.8 6.9 %all-to-all-start.3 = ((f32[2,4,128]{2,0,1:T(2,128)}), f32[2,4,128]{2,0,1:T(2,128)S(1)}, u32[]{:S(2)}, u32[]{:S(2)}) async-start(f32[2,4,128]{2,0,1:T(2,128)} %copy.519), calls=%async_computation.3 | async-start | bytes 8192 | tf_op jit(solution)/shard_map/all_to_all | solution.py:187
  140.6 9.1 %all-to-all-start.9 = ((f32[2,256,128]{2,0,1:T(2,128)}), f32[2,256,128]{2,0,1:T(2,128)S(1)}, u32[]{:S(2)}, u32[]{:S(2)}) async-start(f32[2,256,128]{2,0,1:T(2,128)} %copy.552), calls=%async_computation.9 | async-start | bytes 524288 | tf_op jit(solution)/shard_map/all_to_all | solution.py:188
  144.7 11.1 %copy-start.39 = (f32[4,1,128]{2,1,0:T(1,128)S(1)}, f32[4,1,128]{2,1,0:T(1,128)}, u32[]{:S(2)}) copy-start(f32[4,1,128]{2,1,0:T(1,128)} %copy-done.38) | copy-start | bytes 6148
  149.7 12.3 %all-to-all-start.8 = ((f32[2,512,128]{2,0,1:T(2,128)}), f32[2,512,128]{2,0,1:T(2,128)S(1)}, u32[]{:S(2)}, u32[]{:S(2)}) async-start(f32[2,512,128]{2,0,1:T(2,128)} %copy.545), calls=%async_computation.8 | async-start | bytes 1048576 | tf_op jit(solution)/shard_map/all_to_all | solution.py:188
  163.5 2.7 %copy-start.11 = (bf16[8,256,128]{2,0,1:T(8,128)(2,1)S(1)}, bf16[8,256,128]{2,0,1:T(8,128)(2,1)}, u32[]{:S(2)}) copy-start(bf16[8,256,128]{2,0,1:T(8,128)(2,1)} %fusion.154) | copy-start | bytes 1572868
  163.5 2.7 %copy-start.12 = (bf16[8,256,128]{2,0,1:T(8,128)(2,1)S(1)}, bf16[8,256,128]{2,0,1:T(8,128)(2,1)}, u32[]{:S(2)}) copy-start(bf16[8,256,128]{2,0,1:T(8,128)(2,1)} %fusion.155) | copy-start | bytes 1572868
  177.3 3.5 %copy-start.15 = (f32[8,256,256]{1,2,0:T(8,128)S(1)}, f32[8,256,256]{1,2,0:T(8,128)}, u32[]{:S(2)}) copy-start(f32[8,256,256]{1,2,0:T(8,128)} %copy-done.14) | copy-start | bytes 6291460
  186.6 3.8 %copy-start.16 = (bf16[8,1024,128]{2,1,0:T(8,128)(2,1)}, bf16[8,1024,128]{2,1,0:T(8,128)(2,1)S(1)}, u32[]{:S(2)}) copy-start(bf16[8,1024,128]{2,1,0:T(8,128)(2,1)S(1)} %copy.488) | copy-start | bytes 6291460
  190.5 5.4 %copy-start.40 = (pred[2]{0:T(512)(128)(4,1)S(1)}, pred[2]{0:T(512)(128)(4,1)}, u32[]{:S(2)}) copy-start(pred[2]{0:T(512)(128)(4,1)} %get-tuple-element.94) | copy-start | bytes 10
  195.8 4.3 %copy-start.17 = (bf16[8,1024,128]{2,1,0:T(8,128)(2,1)S(1)}, bf16[8,1024,128]{2,1,0:T(8,128)(2,1)}, u32[]{:S(2)}) copy-start(bf16[8,1024,128]{2,1,0:T(8,128)(2,1)} %copy-done.16) | copy-start | bytes 6291460
  195.8 4.3 %copy-start.41 = (pred[2]{0:T(512)(128)(4,1)S(1)}, pred[2]{0:T(512)(128)(4,1)}, u32[]{:S(2)}) copy-start(pred[2]{0:T(512)(128)(4,1)} %compare_and_fusion.4) | copy-start | bytes 10
  200.1 3.2 %copy-start.1 = (f32[8,2,256,256]{2,3,1,0:T(8,128)S(1)}, f32[8,2,256,256]{2,3,1,0:T(8,128)}, u32[]{:S(2)}) copy-start(f32[8,2,256,256]{2,3,1,0:T(8,128)} %copy.501) | copy-start | bytes 12582916
  200.1 4.4 %copy-start.5 = (bf16[8,1024,128]{2,1,0:T(8,128)(2,1)S(1)}, bf16[8,1024,128]{2,1,0:T(8,128)(2,1)}, u32[]{:S(2)}) copy-start(bf16[8,1024,128]{2,1,0:T(8,128)(2,1)} %copy.497) | copy-start | bytes 6291460
  201.0 5.9 %copy-start.10 = (f32[8,2,256,256]{3,2,1,0:T(8,128)}, f32[8,2,256,256]{3,2,1,0:T(8,128)S(1)}, u32[]{:S(2)}) copy-start(f32[8,2,256,256]{3,2,1,0:T(8,128)S(1)} %get-tuple-element.74) | copy-start | bytes 12582916
  214.9 6.1 %copy-start = (f32[8,2,256,256]{2,3,1,0:T(8,128)S(1)}, f32[8,2,256,256]{2,3,1,0:T(8,128)}, u32[]{:S(2)}) copy-start(f32[8,2,256,256]{2,3,1,0:T(8,128)} %copy.499) | copy-start | bytes 12582916
  214.9 6.5 %copy-start.6 = (bf16[8,1024,128]{2,1,0:T(8,128)(2,1)S(1)}, bf16[8,1024,128]{2,1,0:T(8,128)(2,1)}, u32[]{:S(2)}) copy-start(bf16[8,1024,128]{2,1,0:T(8,128)(2,1)} %copy.497) | copy-start | bytes 6291460
  214.9 7.1 %copy-start.7 = (f32[8,2,256,128]{3,2,1,0:T(8,128)S(1)}, f32[8,2,256,128]{3,2,1,0:T(8,128)}, u32[]{:S(2)}) copy-start(f32[8,2,256,128]{3,2,1,0:T(8,128)} %fusion.10) | copy-start | bytes 6291460
  214.9 7.7 %copy-start.19 = (f32[8,2,256,128]{3,2,1,0:T(8,128)S(1)}, f32[8,2,256,128]{3,2,1,0:T(8,128)}, u32[]{:S(2)}) copy-start(f32[8,2,256,128]{3,2,1,0:T(8,128)} %fusion.8) | copy-start | bytes 6291460
  222.7 1.7 copy-start.25
  222.7 1.7 copy-start.37
  (15 other events, 19.3 us)
where the time goes:
time: 233 us; the launch traced here: 230 us
  starting transfers between devices  73.8 us (32%)
  local copies, waits for them, and re-layouts  57.8 us (25%)
  other arithmetic  36.1 us (15%)
  waiting for transfers between devices  35 us (15%)
  matrix products  25.8 us (11%)
    ppermute x8, starting transfers between devices, from_behind(): lax.ppermute(value, axis, [(source, source + steps) for source in range(i...  21.8 us
    dot_general x9, matrix products, block_terms(): jnp.einsum('hgqk,hgkd->hgqd', weights.astype(jnp.bfloat16), value_grp[:,...  13.8 us
    unnamed x95, local copies, waits for them, and re-layouts  12.3 us
    dot_general x9, matrix products, block_terms(): jnp.einsum('hgqd,hgkd->hgqk', query_grp, key_grp[:, offset:offset + group...  12.1 us
    all_to_all x2, waiting for transfers between devices, local(): lax.all_to_all(query_rows, 'grp', split_axis=0, concat_axis=1, tiled=True)  11.8 us
    all_to_all x2, starting transfers between devices, local(): lax.all_to_all(value_rows, 'grp', split_axis=0, concat_axis=1, tiled=True)  11 us
    all_to_all x2, waiting for transfers between devices, local(): lax.all_to_all(value_rows, 'grp', split_axis=0, concat_axis=1, tiled=True)  10.8 us
    select_n x2, local copies, waits for them, and re-layouts, block_terms(): masked = jnp.where(allowed, scores, very_negative)  10.7 us
  transfers between devices with their start and end apart: 20, of which 10 were waited for; matrix products, arithmetic and copies ran while one was open for 29% of the time, Pallas kernels for 0%

commit v1 on v0

v1 whole, which is shorter than its diff:
```python
import math

import jax
import jax.numpy as jnp
from jax import lax
from jax.experimental import pallas as pl
from jax.experimental.pallas import tpu as pltpu
from jax.sharding import PartitionSpec as P

HEADS = 8
DIM = 128
BLK = 256
SLAB = 32
ROWS = 512
COLS = HEADS * DIM
NEG = -1e30
RATE = math.log2(math.e) / math.sqrt(DIM)
MESH = pl.DeviceIdType.MESH
BF = jnp.bfloat16
F32 = jnp.float32


def fold(value, factor):
    rows, width = value.shape
    paired = value.astype(F32).reshape(rows // (2 * SLAB), 2, SLAB, width)
    summed = paired[:, 0] + paired[:, 1]
    return (summed * factor).reshape(rows // 2, width).astype(BF)


def spread(value, times):
    rows, width = value.shape
    wide = jnp.broadcast_to(
        value.reshape(rows // SLAB, 1, SLAB, width), (rows // SLAB, times, SLAB, width)
    )
    return wide.reshape(rows * times, width)


def attend(query, keys, values, weight, bias=None):
    scores = lax.dot_general(
        query, keys, (((1,), (1,)), ((), ())), preferred_element_type=F32
    )
    if bias is not None:
        scores = scores + bias
    peak = jnp.max(scores, axis=1, keepdims=True)
    probs = jnp.exp2((scores - peak) * RATE).astype(BF)
    tail = jnp.full((values.shape[0], DIM), weight, BF)
    both = jnp.dot(probs, jnp.concatenate([values, tail], axis=1), preferred_element_type=F32)
    return jnp.broadcast_to(peak, (peak.shape[0], DIM)), both


def kernel(
    count,
    q_hbm,
    k_hbm,
    v_hbm,
    o_hbm,
    q0,
    kv0,
    qs,
    q1,
    q2,
    q3,
    kv1,
    kv3,
    perm,
    back,
    far0,
    far1,
    near0,
    near1,
    n2,
    x2,
    p2,
    px,
    x3,
    p3,
    acc,
    top,
    out,
    in_sem,
    halo0_send,
    halo0_recv,
    halo1_send,
    halo1_recv,
    n2_send,
    n2_recv,
    px_send,
    px_recv,
    x3_send,
    x3_recv,
    p3_send,
    p3_recv,
    out_sem,
):
    groups = count // 4
    seq = lax.axis_index("seq")
    grp = lax.axis_index("grp")
    me = seq * 4 + grp
    odd = grp % 2
    high = grp // 2

    def spot(index):
        wrapped = (index + count) % count
        return (wrapped // 4, wrapped % 4)

    far_dev = spot(me - 1 + 2 * odd)
    near_dev = spot(me + 1 - 2 * odd)
    skip_to = spot(me - 4 + 8 * odd)
    seq_prev = ((seq + groups - 1) % groups, grp)
    seq_next = ((seq + 1) % groups, grp)
    cross_dev = ((seq + groups + 1 - 2 * high) % groups, 3 - grp)

    loads = [
        pltpu.make_async_copy(k_hbm, kv0.at[0], in_sem.at[0]),
        pltpu.make_async_copy(v_hbm, kv0.at[1], in_sem.at[1]),
        pltpu.make_async_copy(q_hbm, q0, in_sem.at[2]),
    ]
    for load in loads:
        load.start()

    barrier = pltpu.get_barrier_semaphore()
    others = (far_dev, near_dev, seq_prev, seq_next, cross_dev)
    for other in others:
        pl.semaphore_signal(barrier, inc=1, device_id=other, device_id_type=MESH)

    row = lax.broadcasted_iota(jnp.int32, (BLK, BLK), 0)
    col = lax.broadcasted_iota(jnp.int32, (BLK, BLK), 1)
    perm[...] = jnp.where((row % SLAB) * 8 + row // SLAB == col, 1.0, 0.0).astype(BF)
    back[...] = jnp.where((col % SLAB) * 8 + col // SLAB == row, 1.0, 0.0).astype(BF)

    far_blk = odd
    near_blk = 1 - odd

    def columns(head):
        return pl.ds(pl.multiple_of(head * DIM, DIM), DIM)

    def halo0(side, kv, head):
        blk = (far_blk, near_blk)[side]
        return pltpu.make_async_remote_copy(
            src_ref=kv0.at[kv, pl.ds(pl.multiple_of(blk * BLK, BLK), BLK), columns(head)],
            dst_ref=(far0, near0)[side].at[head, kv],
            send_sem=halo0_send.at[side, kv, head],
            recv_sem=halo0_recv.at[side, kv, head],
            device_id=(far_dev, near_dev)[side],
            device_id_type=MESH,
        )

    def halo1(side, head):
        half = 1 - (far_blk, near_blk)[side]
        return pltpu.make_async_remote_copy(
            src_ref=kv1.at[head, half],
            dst_ref=(far1, near1)[side].at[head],
            send_sem=halo1_send.at[side, head],
            recv_sem=halo1_recv.at[side, head],
            device_id=(far_dev, near_dev)[side],
            device_id_type=MESH,
        )

    def n2_copy(leg, head):
        return pltpu.make_async_remote_copy(
            src_ref=n2.at[head],
            dst_ref=(p2, x2)[leg].at[head],
            send_sem=n2_send.at[leg, head],
            recv_sem=n2_recv.at[leg, head],
            device_id=(near_dev, skip_to)[leg],
            device_id_type=MESH,
        )

    def px_copy(head):
        return pltpu.make_async_remote_copy(
            src_ref=x2.at[head],
            dst_ref=px.at[head],
            send_sem=px_send.at[head],
            recv_sem=px_recv.at[head],
            device_id=near_dev,
            device_id_type=MESH,
        )

    def x3_copy(slot):
        return pltpu.make_async_remote_copy(
            src_ref=kv3,
            dst_ref=x3.at[slot],
            send_sem=x3_send.at[slot],
            recv_sem=x3_recv.at[slot],
            device_id=(seq_next, seq_prev, cross_dev)[slot],
            device_id_type=MESH,
        )

    def p3_copy(slot):
        return pltpu.make_async_remote_copy(
            src_ref=x3.at[slot],
            dst_ref=p3.at[slot],
            send_sem=p3_send.at[slot],
            recv_sem=p3_recv.at[slot],
            device_id=near_dev,
            device_id_type=MESH,
        )

    def out_copy(head):
        return pltpu.make_async_copy(out.at[head], o_hbm.at[:, columns(head)], out_sem.at[head])

    loads[0].wait()
    loads[1].wait()
    pl.semaphore_wait(barrier, len(others))

    for head in range(2):
        for kv in range(2):
            halo0(0, kv, head).start()
    for head in range(2):
        for kv in range(2):
            halo0(1, kv, head).start()

    def coarsen_head(head, carry):
        for kv in range(2):
            factor = (0.5, 1.0)[kv]
            for half in range(2):
                natural = kv0[kv, half * BLK : (half + 1) * BLK, columns(head)]
                slabs = jnp.dot(perm[...], natural, preferred_element_type=F32)
                first = fold(slabs, factor)
                kv1[head, half, kv] = first
                third = fold(fold(first, factor), factor)
                kv3[kv, head, half * SLAB : (half + 1) * SLAB, :] = third
        return carry

    lax.fori_loop(0, HEADS, coarsen_head, 0)

    for slot in range(3):
        x3_copy(slot).start()

    def send_head(head, carry):
        for side in range(2):
            halo1(side, head).start()

        @pl.when(head < HEADS - 2)
        def _():
            for side in range(2):
                for kv in range(2):
                    halo0(side, kv, head + 2).start()

        return carry

    lax.fori_loop(0, HEADS, send_head, 0)

    loads[2].wait()

    def query_head(head, carry):
        for half in range(2):
            natural = q0[half * BLK : (half + 1) * BLK, columns(head)]
            slabs = jnp.dot(perm[...], natural, preferred_element_type=F32)
            qs[head, half * BLK : (half + 1) * BLK, :] = slabs.astype(BF)
            first = fold(slabs, 0.5)
            second = fold(first, 0.5)
            third = fold(second, 0.5)
            q1[head, half] = first
            q2[head, half * 64 : (half + 1) * 64, :] = second
            q3[head, half * SLAB : (half + 1) * SLAB, :] = third
        return carry

    lax.fori_loop(0, HEADS, query_head, 0)

    def merge(head, start, rows, peak, both):
        where = pl.ds(pl.multiple_of(start, SLAB), rows)
        old = top[head, where, :]
        new = jnp.maximum(old, peak)
        old_scale = jnp.exp2((old - new) * RATE)
        new_scale = jnp.exp2((peak - new) * RATE)
        acc[head, where, :DIM] = acc[head, where, :DIM] * old_scale + both[:, :DIM] * new_scale
        acc[head, where, DIM:] = acc[head, where, DIM:] * old_scale + both[:, DIM:] * new_scale
        top[head, where, :] = new

    def side_terms(head, blk, fine, coarse, bias):
        keys, values = fine[head, 0], fine[head, 1]
        sums_k = fold(jnp.dot(perm[...], keys, preferred_element_type=F32), 0.5)
        sums_v = fold(jnp.dot(perm[...], values, preferred_element_type=F32), 1.0)
        start = blk * BLK
        query = qs[head, pl.ds(pl.multiple_of(start, BLK), BLK), :]
        peak, both = attend(query, keys, values, 1.0)
        merge(head, start, BLK, peak + bias, both)
        rest_k, rest_v = coarse[head, 0], coarse[head, 1]
        peak, both = attend(q1[head, blk], rest_k, rest_v, 2.0)
        merge(head, start, BLK, spread(peak + bias, 2), spread(both, 2))
        peak, both = attend(
            q1[head, 1 - blk],
            jnp.concatenate([rest_k, sums_k], axis=0),
            jnp.concatenate([rest_v, sums_v], axis=0),
            2.0,
        )
        merge(head, (1 - blk) * BLK, BLK, spread(peak + bias, 2), spread(both, 2))
        return sums_k, sums_v

    def own_head(head, carry):
        keys = kv0[0, :, columns(head)]
        values = kv0[1, :, columns(head)]
        for part in range(4):
            where = slice(part * 128, (part + 1) * 128)
            peak, both = attend(qs[head, where, :], keys, values, 1.0)
            acc[head, where, :] = both
            top[head, where, :] = peak
        halo0(1, 0, head).wait_recv()
        halo0(1, 1, head).wait_recv()
        halo1(1, head).wait_recv()
        side_terms(head, near_blk, near0, near1, 0.0)
        return carry

    lax.fori_loop(0, HEADS, own_head, 0)

    for slot in range(3):
        x3_copy(slot).wait_recv()
        p3_copy(slot).start()
    for slot in range(3):
        p3_copy(slot).wait_recv()

    has_prev = jnp.where(seq > 0, 0.0, NEG)
    has_next = jnp.where(seq < groups - 1, 0.0, NEG)
    has_cross = jnp.where(high == 0, has_next, has_prev)

    def third_head(head, carry):
        keys = jnp.concatenate(
            [ref[slot, 0, head] for slot in range(3) for ref in (x3, p3)], axis=0
        )
        values = jnp.concatenate(
            [ref[slot, 1, head] for slot in range(3) for ref in (x3, p3)], axis=0
        )
        place = lax.broadcasted_iota(jnp.int32, (1, 3 * DIM), 1) // DIM
        bias = jnp.where(place == 0, has_prev, jnp.where(place == 1, has_next, has_cross))
        peak, both = attend(q3[head], keys, values, 8.0, bias)
        merge(head, 0, ROWS, spread(peak, 8), spread(both, 8))
        return carry

    lax.fori_loop(0, HEADS, third_head, 0)

    toward = 1 - 2 * odd

    def present(index):
        inside = jnp.logical_and(index >= 0, index < count)
        return jnp.where(inside, 0.0, NEG)

    far_bias = present(me - toward)
    x2_bias = present(me + 3 * toward)
    p2_bias = present(me + 2 * toward)
    px_bias = present(me - 2 * toward)

    def finish(head):
        px_copy(head).wait_recv()
        n2_copy(0, head).wait_recv()
        keys = jnp.concatenate([x2[head, 0], p2[head, 0], px[head, 0]], axis=0)
        values = jnp.concatenate([x2[head, 1], p2[head, 1], px[head, 1]], axis=0)
        place = lax.broadcasted_iota(jnp.int32, (1, 3 * DIM), 1) // DIM
        bias = jnp.where(place == 0, x2_bias, jnp.where(place == 1, p2_bias, px_bias))
        peak, both = attend(q2[head], keys, values, 4.0, bias)
        merge(head, 0, ROWS, spread(peak, 4), spread(both, 4))
        for half in range(2):
            where = slice(half * BLK, (half + 1) * BLK)
            ratio = (acc[head, where, :DIM] / acc[head, where, DIM:]).astype(BF)
            out[head, where, :] = jnp.dot(
                back[...], ratio, preferred_element_type=F32
            ).astype(BF)
        out_copy(head).start()

    def relay(head):
        n2_copy(1, head).wait_recv()
        px_copy(head).start()

    def far_head(head, carry):
        halo0(0, 0, head).wait_recv()
        halo0(0, 1, head).wait_recv()
        halo1(0, head).wait_recv()
        for kv in range(2):
            factor = (0.5, 1.0)[kv]
            slabs = jnp.dot(perm[...], far0[head, kv], preferred_element_type=F32)
            n2[head, kv, 0:64, :] = fold(fold(slabs, factor), factor)
            n2[head, kv, 64:128, :] = fold(far1[head, kv], factor)
        n2_copy(0, head).start()
        n2_copy(1, head).start()

        @pl.when(head > 0)
        def _():
            relay(head - 1)

        side_terms(head, far_blk, far0, far1, far_bias)

        @pl.when(head > 0)
        def _():
            finish(head - 1)

        return carry

    lax.fori_loop(0, HEADS, far_head, 0)
    relay(HEADS - 1)
    finish(HEADS - 1)

    def drain(head, carry):
        for side in range(2):
            for kv in range(2):
                halo0(side, kv, head).wait_send()
            halo1(side, head).wait_send()
        n2_copy(0, head).wait_send()
        n2_copy(1, head).wait_send()
        px_copy(head).wait_send()
        out_copy(head).wait()
        return carry

    lax.fori_loop(0, HEADS, drain, 0)
    for slot in range(3):
        x3_copy(slot).wait_send()
        p3_copy(slot).wait_send()


def solution(mesh):
    count = mesh.shape["seq"] * mesh.shape["grp"]

    def local(query_vecs, key_vecs, value_vecs):
        anywhere = pl.BlockSpec(memory_space=pl.ANY)
        dma = pltpu.SemaphoreType.DMA
        return pl.pallas_call(
            lambda *refs: kernel(count, *refs),
            out_shape=jax.ShapeDtypeStruct((ROWS, COLS), BF),
            in_specs=[anywhere] * 3,
            out_specs=anywhere,
            scratch_shapes=[
                pltpu.VMEM((ROWS, COLS), BF),
                pltpu.VMEM((2, ROWS, COLS), BF),
                pltpu.VMEM((HEADS, ROWS, DIM), BF),
                pltpu.VMEM((HEADS, 2, 128, DIM), BF),
                pltpu.VMEM((HEADS, 128, DIM), BF),
                pltpu.VMEM((HEADS, 64, DIM), BF),
                pltpu.VMEM((HEADS, 2, 2, 128, DIM), BF),
                pltpu.VMEM((2, HEADS, 64, DIM), BF),
                pltpu.VMEM((BLK, BLK), BF),
                pltpu.VMEM((BLK, BLK), BF),
                pltpu.VMEM((HEADS, 2, BLK, DIM), BF),
                pltpu.VMEM((HEADS, 2, 128, DIM), BF),
                pltpu.VMEM((HEADS, 2, BLK, DIM), BF),
                pltpu.VMEM((HEADS, 2, 128, DIM), BF),
                pltpu.VMEM((HEADS, 2, 128, DIM), BF),
                pltpu.VMEM((HEADS, 2, 128, DIM), BF),
                pltpu.VMEM((HEADS, 2, 128, DIM), BF),
                pltpu.VMEM((HEADS, 2, 128, DIM), BF),
                pltpu.VMEM((3, 2, HEADS, 64, DIM), BF),
                pltpu.VMEM((3, 2, HEADS, 64, DIM), BF),
                pltpu.VMEM((HEADS, ROWS, 2 * DIM), F32),
                pltpu.VMEM((HEADS, ROWS, DIM), F32),
                pltpu.VMEM((HEADS, ROWS, DIM), BF),
                dma((3,)),
                dma((2, 2, HEADS)),
                dma((2, 2, HEADS)),
                dma((2, HEADS)),
                dma((2, HEADS)),
                dma((2, HEADS)),
                dma((2, HEADS)),
                dma((HEADS,)),
                dma((HEADS,)),
                dma((3,)),
                dma((3,)),
                dma((3,)),
                dma((3,)),
                dma((HEADS,)),
            ],
            compiler_params=pltpu.CompilerParams(
                collective_id=0, has_side_effects=True, vmem_limit_bytes=48 * 1024 * 1024
            ),
        )(query_vecs, key_vecs, value_vecs)

    spec = P(("seq", "grp"), None)
    return jax.shard_map(
        local, mesh=mesh, in_specs=(spec, spec, spec), out_specs=spec, check_vma=False
    )
```

time: 233 us -> 74 us (0.32)
  the two profiles are of different devices: /device:TPU:97 before, /device:TPU:1 now
where the time goes in v1:
time: 74 us; the launch traced here: 73.8 us
  Pallas kernels  69.1 us (93%)
  local copies, waits for them, and re-layouts  4.65 us (6%)
    pallas_call x1, Pallas kernels, local(): pl.pallas_call(lambda *refs: kernel(count, *refs), out_shape=jax.ShapeDty...  69.1 us
    unnamed x7, local copies, waits for them, and re-layouts  4.65 us

profile of v1, /device:TPU:1, one launch (start us, length us, event | category | flops | bytes accessed | tf_op | source)
XLA Modules:
  0.0 73.8 jit_solution(11784538231283316951)
XLA Ops:
  0.0 0.0 copy-start
  0.0 1.2 %copy-done = bf16[512,1024]{1,0:T(8,128)(2,1)S(1)} copy-done((bf16[512,1024]{1,0:T(8,128)(2,1)S(1)}, bf16[512,1024]{1,0:T(8,128)(2,1)}, u32[]{:S(2)}) %copy-start) | copy-done | bytes 1048600
  1.2 0.0 copy-start.1
  1.2 1.2 %copy-done.1 = bf16[512,1024]{1,0:T(8,128)(2,1)S(1)} copy-done((bf16[512,1024]{1,0:T(8,128)(2,1)S(1)}, bf16[512,1024]{1,0:T(8,128)(2,1)}, u32[]{:S(2)}) %copy-start.1) | copy-done | bytes 1048600
  2.5 0.0 copy-start.2
  2.5 1.2 %copy-done.2 = bf16[512,1024]{1,0:T(8,128)(2,1)S(1)} copy-done((bf16[512,1024]{1,0:T(8,128)(2,1)S(1)}, bf16[512,1024]{1,0:T(8,128)(2,1)}, u32[]{:S(2)}) %copy-start.2) | copy-done | bytes 1048600
  3.7 69.1 %shard_map.37 = bf16[512,1024]{1,0:T(8,128)(2,1)S(1)} custom-call(bf16[512,1024]{1,0:T(8,128)(2,1)S(1)} %copy-done, bf16[512,1024]{1,0:T(8,128)(2,1)S(1)} %copy-done.1, bf16[512,1024]{1,0:T(8,128)(2,1)S(1)} %copy-done.2), custom_call_target="tpu_custom_call" | custom-call | tf_op jit(solution)/shard_map/pallas_call | solution.py:415
  72.8 1.0 %copy.5 = bf16[512,1024]{1,0:T(8,128)(2,1)} copy(bf16[512,1024]{1,0:T(8,128)(2,1)S(1)} %shard_map.37) | data formatting | bytes 2097152
Async XLA Ops:
  0.0 1.2 %copy-start = (bf16[512,1024]{1,0:T(8,128)(2,1)S(1)}, bf16[512,1024]{1,0:T(8,128)(2,1)}, u32[]{:S(2)}) copy-start(bf16[512,1024]{1,0:T(8,128)(2,1)} %refs_0_.1) | copy-start | bytes 3145732
  1.2 1.2 %copy-start.1 = (bf16[512,1024]{1,0:T(8,128)(2,1)S(1)}, bf16[512,1024]{1,0:T(8,128)(2,1)}, u32[]{:S(2)}) copy-start(bf16[512,1024]{1,0:T(8,128)(2,1)} %refs_1_.1) | copy-start | bytes 3145732
  2.5 1.2 %copy-start.2 = (bf16[512,1024]{1,0:T(8,128)(2,1)S(1)}, bf16[512,1024]{1,0:T(8,128)(2,1)}, u32[]{:S(2)}) copy-start(bf16[512,1024]{1,0:T(8,128)(2,1)} %refs_2_.1) | copy-start | bytes 3145732

commit v2 on v1

v2 whole, which is shorter than its diff:
```python
import math

import jax
import jax.numpy as jnp
from jax import lax
from jax.experimental import pallas as pl
from jax.experimental.pallas import tpu as pltpu
from jax.sharding import PartitionSpec as P

HEADS = 8
DIM = 128
BLK = 256
SLAB = 32
ROWS = 512
COLS = HEADS * DIM
NEG = -1e30
RELAY_LAG = 2
FINISH_LAG = 3
WINDOW = 3
RATE = math.log2(math.e) / math.sqrt(DIM)
MESH = pl.DeviceIdType.MESH
BF = jnp.bfloat16
F32 = jnp.float32


def fold(value, factor):
    rows, width = value.shape
    paired = value.astype(F32).reshape(rows // (2 * SLAB), 2, SLAB, width)
    summed = paired[:, 0] + paired[:, 1]
    return (summed * factor).reshape(rows // 2, width).astype(BF)


def spread(value, times):
    rows, width = value.shape
    wide = jnp.broadcast_to(
        value.reshape(rows // SLAB, 1, SLAB, width), (rows // SLAB, times, SLAB, width)
    )
    return wide.reshape(rows * times, width)


def attend(query, parts, weight):
    scores = []
    peak = None
    for keys, _, bias in parts:
        block = lax.dot_general(
            query, keys, (((1,), (1,)), ((), ())), preferred_element_type=F32
        )
        if bias is not None:
            block = block + bias
        scores.append(block)
        for start in range(0, block.shape[1], DIM):
            piece = block[:, start : start + DIM]
            peak = piece if peak is None else jnp.maximum(peak, piece)
    peak = jnp.max(peak, axis=1, keepdims=True)
    both = None
    for block, (_, values, _) in zip(scores, parts):
        probs = jnp.exp2((block - peak) * RATE).astype(BF)
        tail = jnp.full((values.shape[0], DIM), weight, BF)
        term = jnp.dot(
            probs, jnp.concatenate([values, tail], axis=1), preferred_element_type=F32
        )
        both = term if both is None else both + term
    return jnp.broadcast_to(peak, (peak.shape[0], DIM)), both


def when(condition, action):
    if condition is None:
        action()
    else:
        pl.when(condition)(action)


def kernel(
    count,
    q_hbm,
    k_hbm,
    v_hbm,
    o_hbm,
    q0,
    kv0,
    qs,
    q1,
    q2,
    q3,
    kv1,
    kv3,
    perm,
    back,
    far0,
    far1,
    near0,
    near1,
    kv2,
    n2,
    x2,
    p2,
    px,
    x3,
    p3,
    acc,
    top,
    acc1,
    top1,
    out,
    in_sem,
    halo0_send,
    halo0_recv,
    halo1_send,
    halo1_recv,
    n2_send,
    n2_recv,
    px_send,
    px_recv,
    x3_send,
    x3_recv,
    p3_send,
    p3_recv,
    out_sem,
    own_send,
    turn_send,
):
    groups = count // 4
    seq = lax.axis_index("seq")
    grp = lax.axis_index("grp")
    me = seq * 4 + grp
    odd = grp % 2
    high = grp // 2

    def spot(index):
        wrapped = (index + count) % count
        return (wrapped // 4, wrapped % 4)

    far_dev = spot(me - 1 + 2 * odd)
    near_dev = spot(me + 1 - 2 * odd)
    skip_to = spot(me - 4 + 8 * odd)
    direct_dev = spot(me + 3 - 6 * odd)
    mirror_dev = (seq, 3 - grp)
    seq_prev = ((seq + groups - 1) % groups, grp)
    seq_next = ((seq + 1) % groups, grp)
    cross_dev = ((seq + groups + 1 - 2 * high) % groups, 3 - grp)

    loads = [
        pltpu.make_async_copy(k_hbm, kv0.at[0], in_sem.at[0]),
        pltpu.make_async_copy(v_hbm, kv0.at[1], in_sem.at[1]),
        pltpu.make_async_copy(q_hbm, q0, in_sem.at[2]),
    ]
    for load in loads:
        load.start()

    last = groups - 1
    edge = jnp.logical_or(seq == 0, seq == last)
    has_far = jnp.logical_and(me > 0, me < count - 1)
    has_prev = seq > 0
    has_next = seq < last
    has_cross = jnp.where(high == 0, seq < last, seq > 0)
    wrap_next = jnp.logical_and(seq % 4 == 3, has_next)
    wrap_prev = jnp.logical_and(seq % 4 == 0, has_prev)
    wraps = jnp.logical_or(wrap_next, wrap_prev)
    turned = jnp.logical_or(
        jnp.logical_and(grp == 2, wrap_next), jnp.logical_and(grp == 1, wrap_prev)
    )
    gives_own = jnp.logical_or(turned, jnp.logical_or(me == 0, me == count - 1))
    meets_own = jnp.logical_or(gives_own, jnp.logical_or(me == 3, me == count - 4))
    inner = jnp.where(odd == 0, seq > 0, seq < last)
    gives_skip = jnp.logical_and(
        inner,
        jnp.logical_not(
            jnp.logical_or(
                jnp.logical_and(grp == 2, wrap_prev), jnp.logical_and(grp == 1, wrap_next)
            )
        ),
    )
    takes_skip = jnp.logical_or(
        jnp.where(odd == 0, seq < last, seq > 0), jnp.logical_or(me == 3, me == count - 4)
    )
    mate_skip = jnp.logical_or(inner, jnp.logical_or(me == 2, me == count - 3))
    gives_turn = jnp.where(high == 0, wrap_next, wrap_prev)
    mate_far = jnp.where(odd == 0, me + 1 < count - 1, me > 1)

    @pl.when(edge)
    def _():
        for ref in (far0, far1, x2, p2, px, x3, p3):
            ref[...] = jnp.zeros_like(ref)

    barrier = pltpu.get_barrier_semaphore()
    links = (
        (far_dev, has_far),
        (near_dev, None),
        (seq_prev, has_prev),
        (seq_next, has_next),
        (cross_dev, has_cross),
        (direct_dev, meets_own),
        (mirror_dev, jnp.logical_and(wraps, odd == high)),
    )
    for other, exists in links:
        when(exists, lambda: pl.semaphore_signal(
            barrier, inc=1, device_id=other, device_id_type=MESH
        ))

    row = lax.broadcasted_iota(jnp.int32, (BLK, BLK), 0)
    col = lax.broadcasted_iota(jnp.int32, (BLK, BLK), 1)
    perm[...] = jnp.where((row % SLAB) * 8 + row // SLAB == col, 1.0, 0.0).astype(BF)
    back[...] = jnp.where((col % SLAB) * 8 + col // SLAB == row, 1.0, 0.0).astype(BF)

    far_blk = odd
    near_blk = 1 - odd

    def columns(head):
        return pl.ds(pl.multiple_of(head * DIM, DIM), DIM)

    def halo0(side, kv, head):
        blk = (far_blk, near_blk)[side]
        return pltpu.make_async_remote_copy(
            src_ref=kv0.at[kv, pl.ds(pl.multiple_of(blk * BLK, BLK), BLK), columns(head)],
            dst_ref=(far0, near0)[side].at[head, kv],
            send_sem=halo0_send.at[side, kv, head],
            recv_sem=halo0_recv.at[side, kv, head],
            device_id=(far_dev, near_dev)[side],
            device_id_type=MESH,
        )

    def halo1(side, head):
        half = 1 - (far_blk, near_blk)[side]
        return pltpu.make_async_remote_copy(
            src_ref=kv1.at[head, half],
            dst_ref=(far1, near1)[side].at[head],
            send_sem=halo1_send.at[side, head],
            recv_sem=halo1_recv.at[side, head],
            device_id=(far_dev, near_dev)[side],
            device_id_type=MESH,
        )

    def n2_copy(leg, head):
        return pltpu.make_async_remote_copy(
            src_ref=n2.at[head],
            dst_ref=(p2, x2)[leg].at[head],
            send_sem=n2_send.at[leg, head],
            recv_sem=n2_recv.at[leg, head],
            device_id=(near_dev, skip_to)[leg],
            device_id_type=MESH,
        )

    def px_copy(head):
        return pltpu.make_async_remote_copy(
            src_ref=x2.at[head],
            dst_ref=px.at[head],
            send_sem=px_send.at[head],
            recv_sem=px_recv.at[head],
            device_id=near_dev,
            device_id_type=MESH,
        )

    def x3_copy(slot):
        return pltpu.make_async_remote_copy(
            src_ref=kv3,
            dst_ref=x3.at[slot],
            send_sem=x3_send.at[slot],
            recv_sem=x3_recv.at[slot],
            device_id=(seq_next, seq_prev, cross_dev)[slot],
            device_id_type=MESH,
        )

    def turn_copy():
        return pltpu.make_async_remote_copy(
            src_ref=x3.at[2],
            dst_ref=x3.at[1 - high],
            send_sem=turn_send,
            recv_sem=x3_recv.at[1 - high],
            device_id=mirror_dev,
            device_id_type=MESH,
        )

    def own_copy(head):
        return pltpu.make_async_remote_copy(
            src_ref=kv2.at[head],
            dst_ref=x2.at[head],
            send_sem=own_send.at[head],
            recv_sem=n2_recv.at[1, head],
            device_id=direct_dev,
            device_id_type=MESH,
        )

    def p3_copy(slot):
        return pltpu.make_async_remote_copy(
            src_ref=x3.at[slot],
            dst_ref=p3.at[slot],
            send_sem=p3_send.at[slot],
            recv_sem=p3_recv.at[slot],
            device_id=near_dev,
            device_id_type=MESH,
        )

    def out_copy(head):
        return pltpu.make_async_copy(out.at[head], o_hbm.at[:, columns(head)], out_sem.at[head])

    loads[0].wait()
    loads[1].wait()
    peers = sum(1 if exists is None else jnp.where(exists, 1, 0) for _, exists in links)
    pl.semaphore_wait(barrier, peers)

    @pl.when(has_far)
    def _():
        for head in range(2):
            for kv in range(2):
                halo0(0, kv, head).start()

    for head in range(2):
        for kv in range(2):
            halo0(1, kv, head).start()

    def pair_columns(pair):
        return pl.ds(pl.multiple_of(pair * 2 * DIM, 2 * DIM), 2 * DIM)

    def coarsen_pair(pair, carry):
        for kv in range(2):
            factor = (0.5, 1.0)[kv]
            for half in range(2):
                natural = kv0[kv, half * BLK : (half + 1) * BLK, pair_columns(pair)]
                slabs = jnp.dot(perm[...], natural, preferred_element_type=F32)
                first = fold(slabs, factor)
                second = fold(first, factor)
                third = fold(second, factor)
                for sub in range(2):
                    head = 2 * pair + sub
                    lanes = slice(sub * DIM, (sub + 1) * DIM)
                    kv1[head, half, kv] = first[:, lanes]
                    kv2[head, kv, half * 64 : (half + 1) * 64, :] = second[:, lanes]
                    kv3[kv, head, half * SLAB : (half + 1) * SLAB, :] = third[:, lanes]
        return carry

    lax.fori_loop(0, HEADS // 2, coarsen_pair, 0)

    third_to = (
        jnp.logical_and(has_next, jnp.logical_not(jnp.logical_and(wrap_next, high == 0))),
        jnp.logical_and(has_prev, jnp.logical_not(jnp.logical_and(wrap_prev, high == 1))),
        has_cross,
    )
    third_from = (has_prev, has_next, has_cross)
    for slot in range(3):
        when(third_to[slot], lambda: x3_copy(slot).start())

    def send_side(side, head):
        for kv in range(2):
            halo0(side, kv, head).start()
        halo1(side, head).start()

    @pl.when(has_far)
    def _():
        halo1(0, 0).start()
        halo1(0, 1).start()
        for head in range(2, WINDOW):
            send_side(0, head)

    @pl.when(gives_own)
    def _():
        lax.fori_loop(0, HEADS, lambda head, c: (own_copy(head).start(), c)[1], 0)

    halo1(1, 0).start()
    halo1(1, 1).start()
    lax.fori_loop(2, HEADS, lambda head, c: (send_side(1, head), c)[1], 0)

    loads[2].wait()

    def query_pair(pair, carry):
        for half in range(2):
            natural = q0[half * BLK : (half + 1) * BLK, pair_columns(pair)]
            slabs = jnp.dot(perm[...], natural, preferred_element_type=F32)
            first = fold(slabs, 0.5)
            second = fold(first, 0.5)
            third = fold(second, 0.5)
            for sub in range(2):
                head = 2 * pair + sub
                lanes = slice(sub * DIM, (sub + 1) * DIM)
                qs[head, half * BLK : (half + 1) * BLK, :] = slabs[:, lanes].astype(BF)
                q1[head, half] = first[:, lanes]
                q2[head, half * 64 : (half + 1) * 64, :] = second[:, lanes]
                q3[head, half * SLAB : (half + 1) * SLAB, :] = third[:, lanes]
        return carry

    lax.fori_loop(0, HEADS // 2, query_pair, 0)

    def hidden(exists):
        return jnp.where(exists, 0.0, NEG)

    far_bias = hidden(has_far)
    x2_bias = hidden(takes_skip)
    p2_bias = hidden(mate_far)
    px_bias = hidden(mate_skip)
    third_bias = [hidden(exists) for exists in third_from]

    def half_rows(blk):
        return pl.ds(pl.multiple_of(blk * BLK, BLK), BLK)

    def fine_levels(head):
        sums = []
        for ref in (far0, near0):
            for kv in range(2):
                slabs = jnp.dot(perm[...], ref[head, kv], preferred_element_type=F32)
                sums.append(fold(slabs, (0.5, 1.0)[kv]))
        own = (kv0[0, :, columns(head)], kv0[1, :, columns(head)], None)
        far = (far0[head, 0], far0[head, 1], far_bias)
        near = (near0[head, 0], near0[head, 1], None)
        for blk, part in ((far_blk, far), (near_blk, near)):
            peak, both = attend(qs[head, half_rows(blk), :], (own, part), 1.0)
            acc[head, half_rows(blk), :] = both
            top[head, half_rows(blk), :] = peak
        far_rest = (far1[head, 0], far1[head, 1], far_bias)
        near_rest = (near1[head, 0], near1[head, 1], None)
        far_sums = (sums[0], sums[1], far_bias)
        near_sums = (sums[2], sums[3], None)
        for blk, part in ((far_blk, near_sums), (near_blk, far_sums)):
            peak, both = attend(q1[head, blk], (far_rest, near_rest, part), 2.0)
            acc1[head, blk] = both
            top1[head, blk] = peak

    def finish(head):
        keys = [ref[slot, 0, head] for slot in range(3) for ref in (x3, p3)]
        values = [ref[slot, 1, head] for slot in range(3) for ref in (x3, p3)]
        peak3, both3 = attend(
            q3[head],
            [
                (
                    jnp.concatenate(keys[2 * slot : 2 * slot + 2], axis=0),
                    jnp.concatenate(values[2 * slot : 2 * slot + 2], axis=0),
                    third_bias[slot],
                )
                for slot in range(3)
            ],
            8.0,
        )
        when(mate_skip, lambda: px_copy(head).wait_recv())
        when(mate_far, lambda: n2_copy(0, head).wait_recv())
        peak2, both2 = attend(
            q2[head],
            [
                (ref[head, 0], ref[head, 1], bias)
                for ref, bias in ((x2, x2_bias), (p2, p2_bias), (px, px_bias))
            ],
            4.0,
        )

        def join(peak_a, both_a, peak_b, both_b):
            peak = jnp.maximum(peak_a, peak_b)
            scale_a = jnp.exp2((peak_a - peak) * RATE)
            scale_b = jnp.exp2((peak_b - peak) * RATE)
            both = jnp.concatenate(
                [
                    both_a[:, :DIM] * scale_a + both_b[:, :DIM] * scale_b,
                    both_a[:, DIM:] * scale_a + both_b[:, DIM:] * scale_b,
                ],
                axis=1,
            )
            return peak, both

        peak2, both2 = join(peak2, both2, spread(peak3, 2), spread(both3, 2))
        for half in range(2):
            rows2 = slice(half * 64, (half + 1) * 64)
            peak1, both1 = join(
                top1[head, half],
                acc1[head, half],
                spread(peak2[rows2], 2),
                spread(both2[rows2], 2),
            )
            rows = slice(half * BLK, (half + 1) * BLK)
            _, both = join(
                top[head, rows, :], acc[head, rows, :], spread(peak1, 2), spread(both1, 2)
            )
            ratio = (both[:, :DIM] / both[:, DIM:]).astype(BF)
            out[head, rows, :] = jnp.dot(
                back[...], ratio, preferred_element_type=F32
            ).astype(BF)
        out_copy(head).start()

    def send_second(head):
        for kv in range(2):
            factor = (0.5, 1.0)[kv]
            slabs = jnp.dot(perm[...], far0[head, kv], preferred_element_type=F32)
            n2[head, kv, 0:64, :] = fold(fold(slabs, factor), factor)
            n2[head, kv, 64:128, :] = fold(far1[head, kv], factor)
        n2_copy(0, head).start()
        when(gives_skip, lambda: n2_copy(1, head).start())

    def relay(head):
        n2_copy(1, head).wait_recv()
        px_copy(head).start()

    def each_head(head, carry):
        @pl.when(has_far)
        def _():
            halo0(0, 0, head).wait_recv()
            halo0(0, 1, head).wait_recv()
            halo1(0, head).wait_recv()
            when(head < HEADS - WINDOW, lambda: send_side(0, head + WINDOW))
            send_second(head)

        when(
            jnp.logical_and(takes_skip, head >= RELAY_LAG), lambda: relay(head - RELAY_LAG)
        )
        halo0(1, 0, head).wait_recv()
        halo0(1, 1, head).wait_recv()
        halo1(1, head).wait_recv()
        fine_levels(head)

        @pl.when(head == FINISH_LAG - 1)
        def _():
            for slot in (2, 0, 1):

                @pl.when(third_from[slot])
                def _():
                    x3_copy(slot).wait_recv()
                    if slot == 2:
                        when(gives_turn, lambda: turn_copy().start())
                    p3_copy(slot).start()

        @pl.when(head == FINISH_LAG)
        def _():
            for slot in range(3):
                when(third_from[slot], lambda: p3_copy(slot).wait_recv())

        @pl.when(head >= FINISH_LAG)
        def _():
            finish(head - FINISH_LAG)

        return carry

    lax.fori_loop(0, HEADS, each_head, 0)

    def trail(head, carry):
        when(
            jnp.logical_and(takes_skip, head + FINISH_LAG - RELAY_LAG < HEADS),
            lambda: relay(head + FINISH_LAG - RELAY_LAG),
        )
        finish(head)
        return carry

    lax.fori_loop(HEADS - FINISH_LAG, HEADS, trail, 0)

    def drain(head, carry):
        @pl.when(has_far)
        def _():
            for kv in range(2):
                halo0(0, kv, head).wait_send()
            halo1(0, head).wait_send()
            n2_copy(0, head).wait_send()

        for kv in range(2):
            halo0(1, kv, head).wait_send()
        halo1(1, head).wait_send()
        when(gives_skip, lambda: n2_copy(1, head).wait_send())
        when(gives_own, lambda: own_copy(head).wait_send())
        when(takes_skip, lambda: px_copy(head).wait_send())
        out_copy(head).wait()
        return carry

    lax.fori_loop(0, HEADS, drain, 0)
    for slot in range(3):
        when(third_to[slot], lambda: x3_copy(slot).wait_send())
        when(third_from[slot], lambda: p3_copy(slot).wait_send())
    when(gives_turn, lambda: turn_copy().wait_send())


def solution(mesh):
    count = mesh.shape["seq"] * mesh.shape["grp"]

    def local(query_vecs, key_vecs, value_vecs):
        anywhere = pl.BlockSpec(memory_space=pl.ANY)
        dma = pltpu.SemaphoreType.DMA
        return pl.pallas_call(
            lambda *refs: kernel(count, *refs),
            out_shape=jax.ShapeDtypeStruct((ROWS, COLS), BF),
            in_specs=[anywhere] * 3,
            out_specs=anywhere,
            scratch_shapes=[
                pltpu.VMEM((ROWS, COLS), BF),
                pltpu.VMEM((2, ROWS, COLS), BF),
                pltpu.VMEM((HEADS, ROWS, DIM), BF),
                pltpu.VMEM((HEADS, 2, 128, DIM), BF),
                pltpu.VMEM((HEADS, 128, DIM), BF),
                pltpu.VMEM((HEADS, 64, DIM), BF),
                pltpu.VMEM((HEADS, 2, 2, 128, DIM), BF),
                pltpu.VMEM((2, HEADS, 64, DIM), BF),
                pltpu.VMEM((BLK, BLK), BF),
                pltpu.VMEM((BLK, BLK), BF),
                pltpu.VMEM((HEADS, 2, BLK, DIM), BF),
                pltpu.VMEM((HEADS, 2, 128, DIM), BF),
                pltpu.VMEM((HEADS, 2, BLK, DIM), BF),
                pltpu.VMEM((HEADS, 2, 128, DIM), BF),
                pltpu.VMEM((HEADS, 2, 128, DIM), BF),
                pltpu.VMEM((HEADS, 2, 128, DIM), BF),
                pltpu.VMEM((HEADS, 2, 128, DIM), BF),
                pltpu.VMEM((HEADS, 2, 128, DIM), BF),
                pltpu.VMEM((HEADS, 2, 128, DIM), BF),
                pltpu.VMEM((3, 2, HEADS, 64, DIM), BF),
                pltpu.VMEM((3, 2, HEADS, 64, DIM), BF),
                pltpu.VMEM((HEADS, ROWS, 2 * DIM), F32),
                pltpu.VMEM((HEADS, ROWS, DIM), F32),
                pltpu.VMEM((HEADS, 2, 128, 2 * DIM), F32),
                pltpu.VMEM((HEADS, 2, 128, DIM), F32),
                pltpu.VMEM((HEADS, ROWS, DIM), BF),
                dma((3,)),
                dma((2, 2, HEADS)),
                dma((2, 2, HEADS)),
                dma((2, HEADS)),
                dma((2, HEADS)),
                dma((2, HEADS)),
                dma((2, HEADS)),
                dma((HEADS,)),
                dma((HEADS,)),
                dma((3,)),
                dma((3,)),
                dma((3,)),
                dma((3,)),
                dma((HEADS,)),
                dma((HEADS,)),
                dma,
            ],
            compiler_params=pltpu.CompilerParams(
                collective_id=0, has_side_effects=True, vmem_limit_bytes=63 * 1024 * 1024
            ),
        )(query_vecs, key_vecs, value_vecs)

    spec = P(("seq", "grp"), None)
    return jax.shard_map(
        local, mesh=mesh, in_specs=(spec, spec, spec), out_specs=spec, check_vma=False
    )
```

time: 74 us -> 63.3 us (0.86)
  the two profiles are of different devices: /device:TPU:1 before, /device:TPU:97 now
where the time goes in v2:
time: 63.3 us; the launch traced here: 63.1 us
  Pallas kernels  60.8 us (96%)
  local copies, waits for them, and re-layouts  2.26 us (4%)
    pallas_call x1, Pallas kernels, local(): pl.pallas_call(lambda *refs: kernel(count, *refs), out_shape=jax.ShapeDty...  60.8 us
    unnamed x1, local copies, waits for them, and re-layouts  2.26 us

profile of v2, /device:TPU:97, one launch (start us, length us, event | category | flops | bytes accessed | tf_op | source)
XLA Modules:
  0.0 63.1 jit_solution(1811079783594361022)
XLA Ops:
  0.0 60.8 %shard_map.37 = bf16[512,1024]{1,0:T(8,128)(2,1)} custom-call(bf16[512,1024]{1,0:T(8,128)(2,1)} %refs_0_.1, bf16[512,1024]{1,0:T(8,128)(2,1)} %refs_1_.1, bf16[512,1024]{1,0:T(8,128)(2,1)} %refs_2_.1), custom_call_target="tpu_custom_call" | custom-call | tf_op jit(solution)/shard_map/pallas_call | solution.py:568
  60.8 2.3 %copy.5 = bf16[512,1024]{1,0:T(8,128)(2,1)} copy(bf16[512,1024]{1,0:T(8,128)(2,1)} %shard_map.37) | data formatting | bytes 2097152

commit v3 on v2

--- a/solution.py
+++ b/solution.py
@@ -15,8 +15,11 @@
 COLS = HEADS * DIM
 NEG = -1e30
 RELAY_LAG = 2
-FINISH_LAG = 3
-WINDOW = 3
+TURN_LAG = 1
+STREAM_LAG = 3
+FINISH_LAG = 4
+DIAGONAL_WINDOW = 3
+STRAIGHT_WINDOW = 5
 RATE = math.log2(math.e) / math.sqrt(DIM)
 MESH = pl.DeviceIdType.MESH
 BF = jnp.bfloat16
@@ -95,6 +98,7 @@
     x2,
     p2,
     px,
+    c3,
     x3,
     p3,
     acc,
@@ -118,6 +122,7 @@
     out_sem,
     own_send,
     turn_send,
+    c3_send,
 ):
     groups = count // 4
     seq = lax.axis_index("seq")
@@ -150,6 +155,7 @@
     last = groups - 1
     edge = jnp.logical_or(seq == 0, seq == last)
     has_far = jnp.logical_and(me > 0, me < count - 1)
+    window = jnp.where(odd == high, DIAGONAL_WINDOW, STRAIGHT_WINDOW)
     has_prev = seq > 0
     has_next = seq < last
     has_cross = jnp.where(high == 0, seq < last, seq > 0)
@@ -175,6 +181,10 @@
     )
     mate_skip = jnp.logical_or(inner, jnp.logical_or(me == 2, me == count - 3))
     gives_turn = jnp.where(high == 0, wrap_next, wrap_prev)
+    flat_next = jnp.logical_and(has_next, seq % 4 != 3)
+    flat_prev = jnp.logical_and(has_prev, seq % 4 != 0)
+    gives_stream = jnp.where(high == 0, flat_prev, flat_next)
+    takes_stream = jnp.where(high == 0, flat_next, flat_prev)
     mate_far = jnp.where(odd == 0, me + 1 < count - 1, me > 1)
 
     @pl.when(edge)
@@ -250,22 +260,41 @@
             device_id_type=MESH,
         )
 
-    def x3_copy(slot):
-        return pltpu.make_async_remote_copy(
-            src_ref=kv3,
-            dst_ref=x3.at[slot],
-            send_sem=x3_send.at[slot],
-            recv_sem=x3_recv.at[slot],
+    stream_dev = spot(me - 4 + 8 * high)
+
+    def c3_copy(head):
+        return pltpu.make_async_remote_copy(
+            src_ref=c3.at[head],
+            dst_ref=x3.at[2, head],
+            send_sem=c3_send.at[head],
+            recv_sem=x3_recv.at[2, head],
+            device_id=stream_dev,
+            device_id_type=MESH,
+        )
+
+    def send_stream(head, part):
+        @pl.when(gives_stream)
+        def _():
+            for kv in range(2):
+                c3[head, kv] = fold(part[head, kv], (0.5, 1.0)[kv])
+            c3_copy(head).start()
+
+    def x3_copy(slot, head):
+        return pltpu.make_async_remote_copy(
+            src_ref=kv3.at[head],
+            dst_ref=x3.at[slot, head],
+            send_sem=x3_send.at[slot, head],
+            recv_sem=x3_recv.at[slot, head],
             device_id=(seq_next, seq_prev, cross_dev)[slot],
             device_id_type=MESH,
         )
 
-    def turn_copy():
-        return pltpu.make_async_remote_copy(
-            src_ref=x3.at[2],
-            dst_ref=x3.at[1 - high],
-            send_sem=turn_send,
-            recv_sem=x3_recv.at[1 - high],
+    def turn_copy(head):
+        return pltpu.make_async_remote_copy(
+            src_ref=x3.at[2, head],
+            dst_ref=x3.at[1 - high, head],
+            send_sem=turn_send.at[head],
+            recv_sem=x3_recv.at[1 - high, head],
             device_id=mirror_dev,
             device_id_type=MESH,
         )
@@ -280,12 +309,12 @@
             device_id_type=MESH,
         )
 
-    def p3_copy(slot):
-        return pltpu.make_async_remote_copy(
-            src_ref=x3.at[slot],
-            dst_ref=p3.at[slot],
-            send_sem=p3_send.at[slot],
-            recv_sem=p3_recv.at[slot],
+    def p3_copy(slot, head):
+        return pltpu.make_async_remote_copy(
+            src_ref=x3.at[slot, head],
+            dst_ref=p3.at[slot, head],
+            send_sem=p3_send.at[slot, head],
+            recv_sem=p3_recv.at[slot, head],
             device_id=near_dev,
             device_id_type=MESH,
         )
@@ -325,7 +354,7 @@
                     lanes = slice(sub * DIM, (sub + 1) * DIM)
                     kv1[head, half, kv] = first[:, lanes]
                     kv2[head, kv, half * 64 : (half + 1) * 64, :] = second[:, lanes]
-                    kv3[kv, head, half * SLAB : (half + 1) * SLAB, :] = third[:, lanes]
+                    kv3[head, kv, half * SLAB : (half + 1) * SLAB, :] = third[:, lanes]
         return carry
 
     lax.fori_loop(0, HEADS // 2, coarsen_pair, 0)
@@ -333,12 +362,9 @@
     third_to = (
         jnp.logical_and(has_next, jnp.logical_not(jnp.logical_and(wrap_next, high == 0))),
         jnp.logical_and(has_prev, jnp.logical_not(jnp.logical_and(wrap_prev, high == 1))),
-        has_cross,
+        gives_turn,
     )
     third_from = (has_prev, has_next, has_cross)
-    for slot in range(3):
-        when(third_to[slot], lambda: x3_copy(slot).start())
-
     def send_side(side, head):
         for kv in range(2):
             halo0(side, kv, head).start()
@@ -348,12 +374,7 @@
     def _():
         halo1(0, 0).start()
         halo1(0, 1).start()
-        for head in range(2, WINDOW):
-            send_side(0, head)
-
-    @pl.when(gives_own)
-    def _():
-        lax.fori_loop(0, HEADS, lambda head, c: (own_copy(head).start(), c)[1], 0)
+        lax.fori_loop(2, window, lambda head, c: (send_side(0, head), c)[1], 0)
 
     halo1(1, 0).start()
     halo1(1, 1).start()
@@ -386,7 +407,7 @@
     x2_bias = hidden(takes_skip)
     p2_bias = hidden(mate_far)
     px_bias = hidden(mate_skip)
-    third_bias = [hidden(exists) for exists in third_from]
+    third_bias = [hidden(exists) for exists in (has_prev, has_next, has_cross)]
 
     def half_rows(blk):
         return pl.ds(pl.multiple_of(blk * BLK, BLK), BLK)
@@ -414,8 +435,10 @@
             top1[head, blk] = peak
 
     def finish(head):
-        keys = [ref[slot, 0, head] for slot in range(3) for ref in (x3, p3)]
-        values = [ref[slot, 1, head] for slot in range(3) for ref in (x3, p3)]
+        for slot in range(3):
+            when(third_from[slot], lambda: p3_copy(slot, head).wait_recv())
+        keys = [ref[slot, head, 0] for slot in range(3) for ref in (x3, p3)]
+        values = [ref[slot, head, 1] for slot in range(3) for ref in (x3, p3)]
         peak3, both3 = attend(
             q3[head],
             [
@@ -479,61 +502,59 @@
             n2[head, kv, 64:128, :] = fold(far1[head, kv], factor)
         n2_copy(0, head).start()
         when(gives_skip, lambda: n2_copy(1, head).start())
+        when(odd != high, lambda: send_stream(head, n2))
 
     def relay(head):
         n2_copy(1, head).wait_recv()
         px_copy(head).start()
-
-    def each_head(head, carry):
-        @pl.when(has_far)
-        def _():
-            halo0(0, 0, head).wait_recv()
-            halo0(0, 1, head).wait_recv()
-            halo1(0, head).wait_recv()
-            when(head < HEADS - WINDOW, lambda: send_side(0, head + WINDOW))
-            send_second(head)
-
+        when(odd == high, lambda: send_stream(head, x2))
+
+    def give_third(head):
+        for slot in range(3):
+            when(third_to[slot], lambda: x3_copy(slot, head).start())
+
+    def turn(head):
+        x3_copy(2, head).wait_recv()
+        turn_copy(head).start()
+
+    def stream(head):
+        awaited = (has_prev, has_next, takes_stream)
+        for slot in range(3):
+            when(awaited[slot], lambda: x3_copy(slot, head).wait_recv())
+            when(third_from[slot], lambda: p3_copy(slot, head).start())
+
+    def during(step, lag, action, exists=None):
+        inside = jnp.logical_and(step >= lag, step < HEADS + lag)
         when(
-            jnp.logical_and(takes_skip, head >= RELAY_LAG), lambda: relay(head - RELAY_LAG)
-        )
+            inside if exists is None else jnp.logical_and(inside, exists),
+            lambda: action(step - lag),
+        )
+
+    def take_far(head):
+        halo0(0, 0, head).wait_recv()
+        halo0(0, 1, head).wait_recv()
+        halo1(0, head).wait_recv()
+        when(head < HEADS - window, lambda: send_side(0, head + window))
+        send_second(head)
+
+    def take_near(head):
         halo0(1, 0, head).wait_recv()
         halo0(1, 1, head).wait_recv()
         halo1(1, head).wait_recv()
         fine_levels(head)
 
-        @pl.when(head == FINISH_LAG - 1)
-        def _():
-            for slot in (2, 0, 1):
-
-                @pl.when(third_from[slot])
-                def _():
-                    x3_copy(slot).wait_recv()
-                    if slot == 2:
-                        when(gives_turn, lambda: turn_copy().start())
-                    p3_copy(slot).start()
-
-        @pl.when(head == FINISH_LAG)
-        def _():
-            for slot in range(3):
-                when(third_from[slot], lambda: p3_copy(slot).wait_recv())
-
-        @pl.when(head >= FINISH_LAG)
-        def _():
-            finish(head - FINISH_LAG)
-
+    def each_step(step, carry):
+        during(step, 0, take_far, has_far)
+        during(step, 0, lambda head: own_copy(head).start(), gives_own)
+        during(step, 0, give_third)
+        during(step, TURN_LAG, turn, gives_turn)
+        during(step, RELAY_LAG, relay, takes_skip)
+        during(step, STREAM_LAG, stream)
+        during(step, 0, take_near)
+        during(step, FINISH_LAG, finish)
         return carry
 
-    lax.fori_loop(0, HEADS, each_head, 0)
-
-    def trail(head, carry):
-        when(
-            jnp.logical_and(takes_skip, head + FINISH_LAG - RELAY_LAG < HEADS),
-            lambda: relay(head + FINISH_LAG - RELAY_LAG),
-        )
-        finish(head)
-        return carry
-
-    lax.fori_loop(HEADS - FINISH_LAG, HEADS, trail, 0)
+    lax.fori_loop(0, HEADS + FINISH_LAG, each_step, 0)
 
     def drain(head, carry):
         @pl.when(has_far)
@@ -548,15 +569,16 @@
         halo1(1, head).wait_send()
         when(gives_skip, lambda: n2_copy(1, head).wait_send())
         when(gives_own, lambda: own_copy(head).wait_send())
+        when(gives_stream, lambda: c3_copy(head).wait_send())
+        when(gives_turn, lambda: turn_copy(head).wait_send())
+        for slot in range(3):
+            when(third_to[slot], lambda: x3_copy(slot, head).wait_send())
+            when(third_from[slot], lambda: p3_copy(slot, head).wait_send())
         when(takes_skip, lambda: px_copy(head).wait_send())
         out_copy(head).wait()
         return carry
 
     lax.fori_loop(0, HEADS, drain, 0)
-    for slot in range(3):
-        when(third_to[slot], lambda: x3_copy(slot).wait_send())
-        when(third_from[slot], lambda: p3_copy(slot).wait_send())
-    when(gives_turn, lambda: turn_copy().wait_send())
 
 
 def solution(mesh):
@@ -578,7 +600,7 @@
                 pltpu.VMEM((HEADS, 128, DIM), BF),
                 pltpu.VMEM((HEADS, 64, DIM), BF),
                 pltpu.VMEM((HEADS, 2, 2, 128, DIM), BF),
-                pltpu.VMEM((2, HEADS, 64, DIM), BF),
+                pltpu.VMEM((HEADS, 2, 64, DIM), BF),
                 pltpu.VMEM((BLK, BLK), BF),
                 pltpu.VMEM((BLK, BLK), BF),
                 pltpu.VMEM((HEADS, 2, BLK, DIM), BF),
@@ -590,8 +612,9 @@
                 pltpu.VMEM((HEADS, 2, 128, DIM), BF),
                 pltpu.VMEM((HEADS, 2, 128, DIM), BF),
                 pltpu.VMEM((HEADS, 2, 128, DIM), BF),
-                pltpu.VMEM((3, 2, HEADS, 64, DIM), BF),
-                pltpu.VMEM((3, 2, HEADS, 64, DIM), BF),
+                pltpu.VMEM((HEADS, 2, 64, DIM), BF),
+                pltpu.VMEM((3, HEADS, 2, 64, DIM), BF),
+                pltpu.VMEM((3, HEADS, 2, 64, DIM), BF),
                 pltpu.VMEM((HEADS, ROWS, 2 * DIM), F32),
                 pltpu.VMEM((HEADS, ROWS, DIM), F32),
                 pltpu.VMEM((HEADS, 2, 128, 2 * DIM), F32),
@@ -606,13 +629,14 @@
                 dma((2, HEADS)),
                 dma((HEADS,)),
                 dma((HEADS,)),
-                dma((3,)),
-                dma((3,)),
-                dma((3,)),
-                dma((3,)),
+                dma((3, HEADS)),
+                dma((3, HEADS)),
+                dma((3, HEADS)),
+                dma((3, HEADS)),
                 dma((HEADS,)),
                 dma((HEADS,)),
-                dma,
+                dma((HEADS,)),
+                dma((HEADS,)),
             ],
             compiler_params=pltpu.CompilerParams(
                 collective_id=0, has_side_effects=True, vmem_limit_bytes=63 * 1024 * 1024

time: 63.3 us -> 61.5 us (0.972); the launches traced: 63.1 us -> 60.3 us
  Pallas kernels: 60.8 us -> 58 us
    pallas_call x1, Pallas kernels: 60.8 us -> 58 us  [local(): pl.pallas_call(lambda *refs: kernel(count, *refs), out_shape=jax.ShapeDty...]
where the time goes in v3:
time: 61.5 us; the launch traced here: 60.3 us
  Pallas kernels  58 us (94%)
  local copies, waits for them, and re-layouts  2.26 us (4%)
    pallas_call x1, Pallas kernels, local(): pl.pallas_call(lambda *refs: kernel(count, *refs), out_shape=jax.ShapeDty...  58 us
    unnamed x1, local copies, waits for them, and re-layouts  2.26 us

profile of v3, /device:TPU:97, one launch (start us, length us, event | category | flops | bytes accessed | tf_op | source)
XLA Modules:
  0.0 60.3 jit_solution(5602763188268594026)
XLA Ops:
  0.0 58.0 %shard_map.37 = bf16[512,1024]{1,0:T(8,128)(2,1)} custom-call(bf16[512,1024]{1,0:T(8,128)(2,1)} %refs_0_.1, bf16[512,1024]{1,0:T(8,128)(2,1)} %refs_1_.1, bf16[512,1024]{1,0:T(8,128)(2,1)} %refs_2_.1), custom_call_target="tpu_custom_call" | custom-call | tf_op jit(solution)/shard_map/pallas_call | solution.py:590
  58.0 2.3 %copy.5 = bf16[512,1024]{1,0:T(8,128)(2,1)} copy(bf16[512,1024]{1,0:T(8,128)(2,1)} %shard_map.37) | data formatting | bytes 2097152

commit v4 on v3

--- a/solution.py
+++ b/solution.py
@@ -99,6 +99,7 @@
     p2,
     px,
     c3,
+    hub,
     x3,
     p3,
     acc,
@@ -123,6 +124,9 @@
     own_send,
     turn_send,
     c3_send,
+    end_send,
+    end_recv,
+    hub_send,
 ):
     groups = count // 4
     seq = lax.axis_index("seq")
@@ -165,8 +169,13 @@
     turned = jnp.logical_or(
         jnp.logical_and(grp == 2, wrap_next), jnp.logical_and(grp == 1, wrap_prev)
     )
-    gives_own = jnp.logical_or(turned, jnp.logical_or(me == 0, me == count - 1))
-    meets_own = jnp.logical_or(gives_own, jnp.logical_or(me == 3, me == count - 4))
+    at_end = jnp.logical_or(me == 0, me == count - 1)
+    is_hub = jnp.logical_or(me == 15, me == count - 16)
+    by_hub = jnp.logical_or(me == 3, me == count - 4)
+    end_dev = spot(jnp.where(at_end, me + jnp.where(me == 0, 15, -15), me + jnp.where(me == 15, -15, 15)))
+    hub_dev = spot(
+        jnp.where(is_hub, me + jnp.where(me == 15, -12, 12), me + jnp.where(me == 3, 12, -12))
+    )
     inner = jnp.where(odd == 0, seq > 0, seq < last)
     gives_skip = jnp.logical_and(
         inner,
@@ -199,7 +208,9 @@
         (seq_prev, has_prev),
         (seq_next, has_next),
         (cross_dev, has_cross),
-        (direct_dev, meets_own),
+        (direct_dev, turned),
+        (end_dev, jnp.logical_or(at_end, is_hub)),
+        (hub_dev, jnp.logical_or(is_hub, by_hub)),
         (mirror_dev, jnp.logical_and(wraps, odd == high)),
     )
     for other, exists in links:
@@ -308,6 +319,30 @@
             device_id=direct_dev,
             device_id_type=MESH,
         )
+
+    def end_copy(head):
+        return pltpu.make_async_remote_copy(
+            src_ref=kv2.at[head],
+            dst_ref=hub.at[head],
+            send_sem=end_send.at[head],
+            recv_sem=end_recv.at[head],
+            device_id=end_dev,
+            device_id_type=MESH,
+        )
+
+    def hub_copy(head):
+        return pltpu.make_async_remote_copy(
+            src_ref=hub.at[head],
+            dst_ref=x2.at[head],
+            send_sem=hub_send.at[head],
+            recv_sem=n2_recv.at[1, head],
+            device_id=hub_dev,
+            device_id_type=MESH,
+        )
+
+    def hand_on(head):
+        end_copy(head).wait_recv()
+        hub_copy(head).start()
 
     def p3_copy(slot, head):
         return pltpu.make_async_remote_copy(
@@ -545,7 +580,9 @@
 
     def each_step(step, carry):
         during(step, 0, take_far, has_far)
-        during(step, 0, lambda head: own_copy(head).start(), gives_own)
+        during(step, 0, lambda head: own_copy(head).start(), turned)
+        during(step, 0, lambda head: end_copy(head).start(), at_end)
+        during(step, TURN_LAG, hand_on, is_hub)
         during(step, 0, give_third)
         during(step, TURN_LAG, turn, gives_turn)
         during(step, RELAY_LAG, relay, takes_skip)
@@ -568,7 +605,9 @@
             halo0(1, kv, head).wait_send()
         halo1(1, head).wait_send()
         when(gives_skip, lambda: n2_copy(1, head).wait_send())
-        when(gives_own, lambda: own_copy(head).wait_send())
+        when(turned, lambda: own_copy(head).wait_send())
+        when(at_end, lambda: end_copy(head).wait_send())
+        when(is_hub, lambda: hub_copy(head).wait_send())
         when(gives_stream, lambda: c3_copy(head).wait_send())
         when(gives_turn, lambda: turn_copy(head).wait_send())
         for slot in range(3):
@@ -613,6 +652,7 @@
                 pltpu.VMEM((HEADS, 2, 128, DIM), BF),
                 pltpu.VMEM((HEADS, 2, 128, DIM), BF),
                 pltpu.VMEM((HEADS, 2, 64, DIM), BF),
+                pltpu.VMEM((HEADS, 2, 128, DIM), BF),
                 pltpu.VMEM((3, HEADS, 2, 64, DIM), BF),
                 pltpu.VMEM((3, HEADS, 2, 64, DIM), BF),
                 pltpu.VMEM((HEADS, ROWS, 2 * DIM), F32),
@@ -637,6 +677,9 @@
                 dma((HEADS,)),
                 dma((HEADS,)),
                 dma((HEADS,)),
+                dma((HEADS,)),
+                dma((HEADS,)),
+                dma((HEADS,)),
             ],
             compiler_params=pltpu.CompilerParams(
                 collective_id=0, has_side_effects=True, vmem_limit_bytes=63 * 1024 * 1024

time: 61.5 us -> 60.7 us (0.987); the launches traced: 60.3 us -> 60.6 us
  no operation moved by 1% of the time
where the time goes in v4:
time: 60.7 us; the launch traced here: 60.6 us
  Pallas kernels  58.3 us (96%)
  local copies, waits for them, and re-layouts  2.26 us (4%)
    pallas_call x1, Pallas kernels, local(): pl.pallas_call(lambda *refs: kernel(count, *refs), out_shape=jax.ShapeDty...  58.3 us
    unnamed x1, local copies, waits for them, and re-layouts  2.26 us

profile of v4, /device:TPU:97, one launch (start us, length us, event | category | flops | bytes accessed | tf_op | source)
XLA Modules:
  0.0 60.6 jit_solution(18039529007864056025)
XLA Ops:
  0.0 58.3 %shard_map.37 = bf16[512,1024]{1,0:T(8,128)(2,1)} custom-call(bf16[512,1024]{1,0:T(8,128)(2,1)} %refs_0_.1, bf16[512,1024]{1,0:T(8,128)(2,1)} %refs_1_.1, bf16[512,1024]{1,0:T(8,128)(2,1)} %refs_2_.1), custom_call_target="tpu_custom_call" | custom-call | tf_op jit(solution)/shard_map/pallas_call | solution.py:629
  58.3 2.3 %copy.5 = bf16[512,1024]{1,0:T(8,128)(2,1)} copy(bf16[512,1024]{1,0:T(8,128)(2,1)} %shard_map.37) | data formatting | bytes 2097152

commit v5 on v4

--- a/solution.py
+++ b/solution.py
@@ -19,7 +19,7 @@
 STREAM_LAG = 3
 FINISH_LAG = 4
 DIAGONAL_WINDOW = 3
-STRAIGHT_WINDOW = 5
+STRAIGHT_WINDOW = 8
 RATE = math.log2(math.e) / math.sqrt(DIM)
 MESH = pl.DeviceIdType.MESH
 BF = jnp.bfloat16

time: 60.7 us -> 60.8 us (level)
  no operation moved by 1% of the time
where the time goes in v5:
time: 60.8 us; the launch traced here: 60.7 us
  Pallas kernels  58.4 us (96%)
  local copies, waits for them, and re-layouts  2.26 us (4%)
    pallas_call x1, Pallas kernels, local(): pl.pallas_call(lambda *refs: kernel(count, *refs), out_shape=jax.ShapeDty...  58.4 us
    unnamed x1, local copies, waits for them, and re-layouts  2.26 us

profile of v5, /device:TPU:97, one launch (start us, length us, event | category | flops | bytes accessed | tf_op | source)
XLA Modules:
  0.0 60.7 jit_solution(10189228625467010897)
XLA Ops:
  0.0 58.4 %shard_map.37 = bf16[512,1024]{1,0:T(8,128)(2,1)} custom-call(bf16[512,1024]{1,0:T(8,128)(2,1)} %refs_0_.1, bf16[512,1024]{1,0:T(8,128)(2,1)} %refs_1_.1, bf16[512,1024]{1,0:T(8,128)(2,1)} %refs_2_.1), custom_call_target="tpu_custom_call" | custom-call | tf_op jit(solution)/shard_map/pallas_call | solution.py:629
  58.4 2.3 %copy.5 = bf16[512,1024]{1,0:T(8,128)(2,1)} copy(bf16[512,1024]{1,0:T(8,128)(2,1)} %shard_map.37) | data formatting | bytes 2097152
